TPU v7x, 256 devices: a whole 4x4x8 slice. The times are simulated.
256 devices in a mesh: img: 32 (over z, y), cls: 8 (over x, core).
Axes of the slice: x: 4, y: 4, z: 8, core: 2. Of those that a mesh axis runs over, the one named last changes fastest.
Arguments:
- embeddings: bfloat16 [3072, 1024], P('img'), may hold values from -128 to 128
- class_text_embedding: bfloat16 [1024, 21888], P(None, 'cls'), may hold values from -1 to 1
- neighbours: int32 [3072, 10], P('img'), may hold values from 0 to 607, as said below
- weights: float32 [3072, 10], P('img'), may hold values from 0.2 to 1
- requests: int32 [32, 32, 16], P('img'), may hold values from -1 to 95, as said below
Outputs:
- labels: float32 [3072, 21888], P('img', 'cls')
Inputs may be any that keep to these rules, and one draw needn't show every extreme that they name: requests[d, p, j] is a row index within device p's 96 rows, or -1 for an empty slot; the live slots of each (d, p) come first; requests[d, d] is empty; every d fills all 16 slots for one p. `neighbours`: a slot of 96 or more names a live request slot of the row's own device.
All inputs are finite; a program needn't handle non-finite values.
Results may differ from a plain program's by a relative error of at most 0.00085.
Values may be sent and summed in bfloat16 or wider, within the bound.
A program may use at most 64 MiB of HBM per device.

v0:
```python
import jax
import jax.numpy as jnp
from jax import lax
from jax.sharding import PartitionSpec as P

LIVE = 21841


smoothing = 1.0


def probabilities(source, class_text_embedding, live):
    logits = jnp.dot(source, class_text_embedding, preferred_element_type=jnp.float32)
    masked = jnp.where(live, logits, -1e30)
    local_top = jnp.max(masked, axis=1)
    top = lax.pmax(local_top, "cls")
    powers = jnp.where(live, jnp.exp(masked - top[:, None]), 0.0)
    total = lax.psum(jnp.sum(powers, axis=1), "cls")
    return powers / total[:, None]


def sweep(extended, first, neighbours, weights):
    acc = jnp.zeros(first.shape, jnp.float32)
    for k in range(neighbours.shape[1]):
        acc = acc + weights[:, k : k + 1] * extended[neighbours[:, k]]
    degree = jnp.sum(weights, axis=1, keepdims=True)
    return (first + smoothing * acc) / (1.0 + smoothing * degree)


def shards(embeddings, class_text_embedding, neighbours, weights, requests):
    width_here = class_text_embedding.shape[1]
    col_start = lax.axis_index("cls") * width_here
    live = (col_start + jnp.arange(width_here) < LIVE)[None, :]
    needed_rows = lax.all_to_all(requests[0], "img", split_axis=0, concat_axis=0, tiled=True)
    picked = jnp.maximum(needed_rows, 0)
    valid = (needed_rows >= 0)[:, :, None]

    def outgoing(table):
        return jnp.where(valid, table[picked], jnp.zeros((), table.dtype))

    first = probabilities(embeddings, class_text_embedding, live)
    arrived = lax.all_to_all(outgoing(first), "img", split_axis=0, concat_axis=0, tiled=True)
    extended = jnp.concatenate([first, arrived.reshape(-1, width_here)], axis=0)
    second = sweep(extended, first, neighbours, weights)
    arrived_two = lax.all_to_all(outgoing(second), "img", split_axis=0, concat_axis=0, tiled=True)
    extended_two = jnp.concatenate([second, arrived_two.reshape(-1, width_here)], axis=0)
    return sweep(extended_two, first, neighbours, weights)


def solution(mesh):
    in_specs = (
        P("img", None),
        P(None, "cls"),
        P("img", None),
        P("img", None),
        P("img", None, None),
    )
    out_specs = P("img", "cls")
    return jax.shard_map(shards, mesh=mesh, in_specs=in_specs, out_specs=out_specs, check_vma=False)
```

profile of v0, /device:TPU:1, one launch (start us, length us, event | category | flops | bytes accessed | tf_op | source)
XLA Modules:
  0.0 464.6 jit_solution(16098481985741856438)
XLA Ops:
  1.4 12.0 %all-to-all-start = ((s32[32,1,16]{2,1,0:T(1,128)}), s32[32,1,16]{2,1,0:T(1,128)S(1)}, u32[]{:S(2)}, u32[]{:S(2)}) async-start(s32[32,1,16]{2,1,0:T(1,128)} %bitcast.1), calls=%async_computation | async-start | bytes 32768 | tf_op jit(solution)/shard_map/all_to_all | solution.py:34
  13.5 4.5 fusion.12
  18.0 12.7 %pmax.7 = f32[96]{0:T(128)S(1)} all-reduce(f32[96]{0:T(128)S(1)} %get-tuple-element.25), channel_id=1, replica_groups=mesh['img'=32,'cls'=8] {'cls'}, use_global_device_ids=true, to_apply=%region_1.2 | all-reduce | flops 96 | bytes 768 | tf_op jit(solution)/shard_map/pmax | solution.py:16
  31.1 14.5 %psum.7 = f32[96]{0:T(128)S(1)} all-reduce(f32[96]{0:T(128)S(1)} %fusion.1), channel_id=1, replica_groups=mesh['img'=32,'cls'=8] {'cls'}, use_global_device_ids=true, to_apply=%region_3.4 | all-reduce | flops 96 | bytes 768 | tf_op jit(solution)/shard_map/psum | solution.py:18
  46.2 4.6 gather_fusion
  50.7 5.6 %broadcast_select_fusion.1 = f32[32,16,2736]{2,1,0:T(8,128)} fusion(f32[32,16,2736]{2,1,0:T(8,128)} %bitcast.52, pred[32,16]{1,0:T(8,128)(4,1)S(1)} %copy.12), kind=kLoop, calls=%fused_computation.26 | loop fusion | flops 1400832 | bytes 11207168 | tf_op jit(solution)/shard_map/jit(_where)/select_n | solution.py:39
  56.3 9.5 %all-to-all-start.1 = ((f32[32,16,2736]{2,1,0:T(8,128)}), f32[32,16,2736]{2,1,0:T(8,128)}, u32[]{:S(2)}, u32[]{:S(2)}) async-start(f32[32,16,2736]{2,1,0:T(8,128)} %broadcast_select_fusion.1), calls=%async_computation.1 | async-start | bytes 11534336 | tf_op jit(solution)/shard_map/all_to_all | solution.py:42
  66.0 125.9 %all-to-all-done.1 = f32[32,16,2736]{2,1,0:T(8,128)} async-done(((f32[32,16,2736]{2,1,0:T(8,128)}), f32[32,16,2736]{2,1,0:T(8,128)}, u32[]{:S(2)}, u32[]{:S(2)}) %all-to-all-start.1) | async-done | bytes 5603360 | tf_op jit(solution)/shard_map/all_to_all | solution.py:42
  191.9 5.9 %pad_maximum_fusion = f32[608,2736]{1,0:T(8,128)} fusion(f32[512,2736]{1,0:T(8,128)} %bitcast.4, f32[96,2736]{1,0:T(8,128)S(1)} %fusion), kind=kLoop, calls=%fused_computation.22 | loop fusion | flops 1663488 | bytes 13307904 | tf_op jit(solution)/shard_map/concatenate | solution.py:43
  197.8 4.4 gather_fusion.1
  202.2 5.3 %gather_fusion.2 = f32[96,2736]{1,0:T(8,128)} fusion(f32[608,2736]{1,0:T(8,128)} %pad_maximum_fusion, s32[1024]{0:T(1024)S(1)} %get-tuple-element.35), kind=kCustom, calls=%fused_computation.2 | custom fusion | bytes 2101632 | tf_op jit(solution)/shard_map/gather | solution.py:25
  207.5 5.3 %gather_fusion.3 = f32[96,2736]{1,0:T(8,128)} fusion(f32[608,2736]{1,0:T(8,128)} %pad_maximum_fusion, s32[1024]{0:T(1024)S(1)} %get-tuple-element.34), kind=kCustom, calls=%fused_computation.3 | custom fusion | bytes 2101632 | tf_op jit(solution)/shard_map/gather | solution.py:25
  212.8 5.4 %gather_fusion.4 = f32[96,2736]{1,0:T(8,128)} fusion(f32[608,2736]{1,0:T(8,128)} %pad_maximum_fusion, s32[1024]{0:T(1024)S(1)} %get-tuple-element.33), kind=kCustom, calls=%fused_computation.4 | custom fusion | bytes 2101632 | tf_op jit(solution)/shard_map/gather | solution.py:25
  218.2 5.3 %gather_fusion.5 = f32[96,2736]{1,0:T(8,128)} fusion(f32[608,2736]{1,0:T(8,128)} %pad_maximum_fusion, s32[1024]{0:T(1024)S(1)} %get-tuple-element.32), kind=kCustom, calls=%fused_computation.5 | custom fusion | bytes 2101632 | tf_op jit(solution)/shard_map/gather | solution.py:25
  223.5 5.3 %gather_fusion.6 = f32[96,2736]{1,0:T(8,128)} fusion(f32[608,2736]{1,0:T(8,128)} %pad_maximum_fusion, s32[1024]{0:T(1024)S(1)} %get-tuple-element.31), kind=kCustom, calls=%fused_computation.6 | custom fusion | bytes 2101632 | tf_op jit(solution)/shard_map/gather | solution.py:25
  228.8 5.3 %gather_fusion.7 = f32[96,2736]{1,0:T(8,128)} fusion(f32[608,2736]{1,0:T(8,128)} %pad_maximum_fusion, s32[1024]{0:T(1024)S(1)} %get-tuple-element.30), kind=kCustom, calls=%fused_computation.7 | custom fusion | bytes 2101632 | tf_op jit(solution)/shard_map/gather | solution.py:25
  234.2 5.4 %gather_fusion.8 = f32[96,2736]{1,0:T(8,128)} fusion(f32[608,2736]{1,0:T(8,128)} %pad_maximum_fusion, s32[1024]{0:T(1024)S(1)} %get-tuple-element.29), kind=kCustom, calls=%fused_computation.8 | custom fusion | bytes 2101632 | tf_op jit(solution)/shard_map/gather | solution.py:25
  239.6 5.3 %gather_fusion.9 = f32[96,2736]{1,0:T(8,128)} fusion(f32[608,2736]{1,0:T(8,128)} %pad_maximum_fusion, s32[1024]{0:T(1024)S(1)} %get-tuple-element.28), kind=kCustom, calls=%fused_computation.9 | custom fusion | bytes 2101632 | tf_op jit(solution)/shard_map/gather | solution.py:25
  244.9 5.3 %gather_fusion.10 = f32[96,2736]{1,0:T(8,128)} fusion(f32[608,2736]{1,0:T(8,128)} %pad_maximum_fusion, s32[1024]{0:T(1024)S(1)} %get-tuple-element.27), kind=kCustom, calls=%fused_computation.10 | custom fusion | bytes 2101632 | tf_op jit(solution)/shard_map/gather | solution.py:25
  250.2 5.2 %add_divide_fusion.1 = f32[96,2736]{1,0:T(8,128)S(1)} fusion(f32[96,2736]{1,0:T(8,128)} %gather_fusion.10, f32[96,2736]{1,0:T(8,128)} %gather_fusion.9, f32[96,2736]{1,0:T(8,128)} %gather_fusion.8, f32[96,2736]{1,0:T(8,128)} %gather_fusion.7, f32[96,2736]{1,0:T(8,128)} %gather_fusion.6, f32[96,2736]{1,0:T(8,128)} %gather_fusion.5, ...), kind=kLoop, calls=%fused_computation.28 | loop fusion | flops 6303744 | bytes 12615216 | tf_op jit(solution)/shard_map/div | solution.py:27
  255.4 4.7 %gather_fusion.11 = f32[512,2736]{1,0:T(8,128)} fusion(f32[96,2736]{1,0:T(8,128)S(1)} %add_divide_fusion.1, s32[1024]{0:T(1024)S(1)} %pad_clamp_fusion.10), kind=kCustom, calls=%fused_computation.11 | custom fusion | bytes 11208704 | tf_op jit(solution)/shard_map/gather | solution.py:39
  263.2 140.8 %all_to_all.19 = f32[32,16,2736]{2,1,0:T(8,128)S(1)} all-to-all(f32[32,16,2736]{2,1,0:T(8,128)S(1)} %broadcast_select_fusion), channel_id=1, replica_groups=mesh['img'=32,'cls'=8] {'img'}, dimensions={0} | all-to-all | bytes 11206656 | tf_op jit(solution)/shard_map/all_to_all | solution.py:45
  411.6 4.4 gather_fusion.13
  416.0 5.3 %gather_fusion.14 = f32[96,2736]{1,0:T(8,128)} fusion(f32[608,2736]{1,0:T(8,128)} %pad_maximum_fusion.1, s32[1024]{0:T(1024)S(1)} %get-tuple-element.34), kind=kCustom, calls=%fused_computation.14 | custom fusion | bytes 2101632 | tf_op jit(solution)/shard_map/gather | solution.py:25
  421.4 5.4 %gather_fusion.15 = f32[96,2736]{1,0:T(8,128)} fusion(f32[608,2736]{1,0:T(8,128)} %pad_maximum_fusion.1, s32[1024]{0:T(1024)S(1)} %get-tuple-element.33), kind=kCustom, calls=%fused_computation.15 | custom fusion | bytes 2101632 | tf_op jit(solution)/shard_map/gather | solution.py:25
  426.7 5.3 %gather_fusion.16 = f32[96,2736]{1,0:T(8,128)} fusion(f32[608,2736]{1,0:T(8,128)} %pad_maximum_fusion.1, s32[1024]{0:T(1024)S(1)} %get-tuple-element.32), kind=kCustom, calls=%fused_computation.16 | custom fusion | bytes 2101632 | tf_op jit(solution)/shard_map/gather | solution.py:25
  432.1 5.3 %gather_fusion.17 = f32[96,2736]{1,0:T(8,128)} fusion(f32[608,2736]{1,0:T(8,128)} %pad_maximum_fusion.1, s32[1024]{0:T(1024)S(1)} %get-tuple-element.31), kind=kCustom, calls=%fused_computation.17 | custom fusion | bytes 2101632 | tf_op jit(solution)/shard_map/gather | solution.py:25
  437.4 5.3 %gather_fusion.18 = f32[96,2736]{1,0:T(8,128)} fusion(f32[608,2736]{1,0:T(8,128)} %pad_maximum_fusion.1, s32[1024]{0:T(1024)S(1)} %get-tuple-element.30), kind=kCustom, calls=%fused_computation.18 | custom fusion | bytes 2101632 | tf_op jit(solution)/shard_map/gather | solution.py:25
  442.7 5.4 %gather_fusion.19 = f32[96,2736]{1,0:T(8,128)} fusion(f32[608,2736]{1,0:T(8,128)} %pad_maximum_fusion.1, s32[1024]{0:T(1024)S(1)} %get-tuple-element.29), kind=kCustom, calls=%fused_computation.19 | custom fusion | bytes 2101632 | tf_op jit(solution)/shard_map/gather | solution.py:25
  448.2 5.3 %gather_fusion.20 = f32[96,2736]{1,0:T(8,128)} fusion(f32[608,2736]{1,0:T(8,128)} %pad_maximum_fusion.1, s32[1024]{0:T(1024)S(1)} %get-tuple-element.28), kind=kCustom, calls=%fused_computation.20 | custom fusion | bytes 2101632 | tf_op jit(solution)/shard_map/gather | solution.py:25
  453.5 5.3 %gather_fusion.21 = f32[96,2736]{1,0:T(8,128)} fusion(f32[608,2736]{1,0:T(8,128)} %pad_maximum_fusion.1, s32[1024]{0:T(1024)S(1)} %get-tuple-element.27), kind=kCustom, calls=%fused_computation.21 | custom fusion | bytes 2101632 | tf_op jit(solution)/shard_map/gather | solution.py:25
  458.8 5.8 %add_divide_fusion = f32[96,2736]{1,0:T(8,128)} fusion(f32[96,2736]{1,0:T(8,128)} %gather_fusion.21, f32[96,2736]{1,0:T(8,128)} %gather_fusion.20, f32[96,2736]{1,0:T(8,128)} %gather_fusion.19, f32[96,2736]{1,0:T(8,128)} %gather_fusion.18, f32[96,2736]{1,0:T(8,128)} %gather_fusion.17, f32[96,2736]{1,0:T(8,128)} %gather_fusion.16, ...), kind=kLoop, calls=%fused_computation.27 | loop fusion | flops 6303744 | bytes 12615216 | tf_op jit(solution)/shard_map/div | solution.py:27
  (32 shorter events, 13.2 us)
Async XLA Ops:
  0.0 13.5 %copy-start = (bf16[96,1024]{1,0:T(8,128)(2,1)S(1)}, bf16[96,1024]{1,0:T(8,128)(2,1)}, u32[]{:S(2)}) copy-start(bf16[96,1024]{1,0:T(8,128)(2,1)} %param.5) | copy-start | bytes 589828
  1.4 44.4 %all-to-all-start = ((s32[32,1,16]{2,1,0:T(1,128)}), s32[32,1,16]{2,1,0:T(1,128)S(1)}, u32[]{:S(2)}, u32[]{:S(2)}) async-start(s32[32,1,16]{2,1,0:T(1,128)} %bitcast.1), calls=%async_computation | async-start | bytes 32768 | tf_op jit(solution)/shard_map/all_to_all | solution.py:34
  56.3 9.5 %copy-start.2 = (f32[96,10]{0,1:T(8,128)S(1)}, f32[96,10]{0,1:T(8,128)}, u32[]{:S(2)}) copy-start(f32[96,10]{0,1:T(8,128)} %param.8) | copy-start | bytes 11524
  56.3 9.6 %copy-start.3 = (s32[96,10]{0,1:T(8,128)S(1)}, s32[96,10]{0,1:T(8,128)}, u32[]{:S(2)}) copy-start(s32[96,10]{0,1:T(8,128)} %param.7) | copy-start | bytes 11524
  56.3 135.6 %all-to-all-start.1 = ((f32[32,16,2736]{2,1,0:T(8,128)}), f32[32,16,2736]{2,1,0:T(8,128)}, u32[]{:S(2)}, u32[]{:S(2)}) async-start(f32[32,16,2736]{2,1,0:T(8,128)} %broadcast_select_fusion.1), calls=%async_computation.1 | async-start | bytes 11534336 | tf_op jit(solution)/shard_map/all_to_all | solution.py:42
  458.8 5.8 %copy-start.1 = (bf16[96,1024]{1,0:T(8,128)(2,1)S(1)}, bf16[96,1024]{1,0:T(8,128)(2,1)}, u32[]{:S(2)}) copy-start(bf16[96,1024]{1,0:T(8,128)(2,1)} %param.5) | copy-start | bytes 589828
where the time goes:
time: 468 us; the launch traced here: 465 us
  blocking collectives  168 us (36%)
  waiting for transfers between devices  126 us (27%)
  local copies, waits for them, and re-layouts  115 us (25%)
  other arithmetic  29.4 us (6%)
  starting transfers between devices  21.5 us (5%)
    all_to_all x1, blocking collectives, shards(): lax.all_to_all(outgoing(second), 'img', split_axis=0, concat_axis=0, tile...  141 us
    all_to_all x1, waiting for transfers between devices, shards(): lax.all_to_all(outgoing(first), 'img', split_axis=0, concat_axis=0, tiled...  126 us
    gather x20, local copies, waits for them, and re-layouts, sweep(): acc = acc + weights[:, k:k + 1] * extended[neighbours[:, k]]  104 us
    psum x1, blocking collectives, probabilities(): total = lax.psum(jnp.sum(powers, axis=1), 'cls')  14.5 us
    pmax x1, blocking collectives, probabilities(): top = lax.pmax(local_top, 'cls')  12.7 us
    all_to_all x1, starting transfers between devices, shards(): lax.all_to_all(requests[0], 'img', split_axis=0, concat_axis=0, tiled=True)  12 us
    div x2, other arithmetic, sweep(): return (first + smoothing * acc) / (1.0 + smoothing * degree)  11 us
    all_to_all x1, starting transfers between devices, shards(): lax.all_to_all(outgoing(first), 'img', split_axis=0, concat_axis=0, tiled...  9.51 us
  transfers between devices with their start and end apart: 2, of which 1 were waited for; matrix products, arithmetic and copies ran while one was open for 1% of the time, Pallas kernels for 0%

commit v1 on v0

v1 whole, which is shorter than its diff:
```python
import functools
import jax
import jax.numpy as jnp
from jax import lax
from jax.experimental import pallas as pl
from jax.experimental.pallas import tpu as pltpu
from jax.sharding import PartitionSpec as P

LIVE = 21841
ROWS = 96
K = 10
CAP = 16
PEERS = 32
ALL = ROWS * PEERS
D = 1024
N = 2736
TN = 256
CHUNK = 512
CHUNKS = ALL // CHUNK
SLOTS = K * 12
F32 = jnp.float32
BF16 = jnp.bfloat16


def dot(a, b):
    return jnp.dot(a, b, preferred_element_type=F32)


def split(x):
    hi = x.astype(BF16)
    return hi, (x - hi.astype(F32)).astype(BF16)


def place(peer, row):
    return peer * ROWS + row


def build_matrix(me, table, peer_ref, row_ref, w_ref, got, list_a, list_b, list_v, dense, m_ref):
    pos = place(peer_ref[...], row_ref[...])
    got[...] = jnp.zeros_like(got)

    def gather(step, carry):
        base = pl.multiple_of(step * 256, 256)
        lanes = lax.broadcasted_iota(jnp.int32, (ROWS, 256), 1) + base
        hot = [jnp.where(lanes == pos[:, k : k + 1], 1.0, 0.0).astype(BF16) for k in range(K)]
        got[...] += dot(jnp.concatenate(hot, axis=0), table(base, 256))
        return carry

    lax.fori_loop(0, ALL // 256, gather, 0)
    lanes = lax.broadcasted_iota(jnp.int32, (ROWS, 128), 1)
    w = w_ref[...]
    scale = 1.0 / (1.0 + jnp.sum(w, axis=1, keepdims=True))
    peers = jnp.zeros((ROWS, 128), F32)
    rows = jnp.zeros((ROWS, 128), F32)
    values = jnp.zeros((ROWS, 128), F32)
    for k in range(K):
        g = got[k * ROWS : (k + 1) * ROWS, :]
        live = lanes < K + 1
        value = (pltpu.roll(g, 128 - 32, 1) + pltpu.roll(g, 128 - 48, 1)) * w[:, k : k + 1]
        take = [g, pltpu.roll(g, 128 - 16, 1), value]
        take = [jnp.where(live, t, 0.0) for t in take]
        if k:
            take = [pltpu.roll(t, 12 * k, 1) for t in take]
        peers, rows, values = peers + take[0], rows + take[1], values + take[2]
    own = lanes == SLOTS
    peers = jnp.where(own, me.astype(F32), peers).astype(jnp.int32)
    rows = jnp.where(own, lax.broadcasted_iota(jnp.int32, (ROWS, 128), 0), rows.astype(jnp.int32))
    where = place(peers, rows)
    list_a[...] = where >> 7
    list_b[...] = where & 127
    list_v[...] = jnp.where(own, 1.0, values) * scale

    def scatter(r, carry):
        a, b, v = list_a[pl.ds(r, 1), :], list_b[pl.ds(r, 1), :], list_v[pl.ds(r, 1), :]
        left = jnp.where(lax.broadcasted_iota(jnp.int32, (32, 128), 0) == a, v, 0.0)
        right = jnp.where(lax.broadcasted_iota(jnp.int32, (128, 128), 0) == b, 1.0, 0.0).astype(BF16)
        both = jnp.concatenate(split(left), axis=0)
        out = lax.dot_general(both, right, (((1,), (1,)), ((), ())), preferred_element_type=F32)
        dense[pl.ds(r, 24, stride=ROWS), :] = out[:24] + out[32:56]
        return carry

    lax.fori_loop(0, ROWS, scatter, 0, unroll=8)
    per = CHUNK // 128
    for i in range(CHUNKS):
        block = jnp.concatenate([dense[(per * i + j) * ROWS : (per * i + j + 1) * ROWS, :] for j in range(per)], axis=1)
        hi, lo = split(block)
        m_ref[i, :ROWS] = hi
        m_ref[i, ROWS:] = lo


def tiles():
    return [(off, min(TN, N - off)) for off in range(0, N, TN)]


def logits_tile(e_ref, c_ref, buf, chunk, slot, off, width):
    rows = pl.ds(pl.multiple_of(chunk * CHUNK, CHUNK), CHUNK)
    buf[slot, :, off : off + width] = dot(e_ref[rows, :D], c_ref[:, off : off + width])


def label_tile(lse_ref, m_ref, buf, acc, chunk, slot, off, width):
    rows = pl.ds(pl.multiple_of(chunk * CHUNK, CHUNK), CHUNK)
    lse = lse_ref[rows, :]
    lse = jnp.concatenate([lse] * (-(-width // 128)), axis=1)[:, :width]
    hi, lo = split(jnp.exp(buf[slot, :, off : off + width] - lse))
    m = m_ref[chunk]
    a = dot(m, hi)
    acc[:, off : off + width] += a[:ROWS] + a[ROWS:] + dot(m[:ROWS], lo)


def kernel(e_ref, c_ref, lse_ref, peer_ref, row_ref, w_ref, o_ref, buf, acc, got, list_a, list_b, list_v, dense, m_ref):
    me = lax.axis_index("img")
    build_matrix(me, lambda base, n: e_ref[pl.ds(base, n), D:], peer_ref, row_ref, w_ref, got, list_a, list_b, list_v, dense, m_ref)
    acc[...] = jnp.zeros_like(acc)
    for off, width in tiles():
        logits_tile(e_ref, c_ref, buf, 0, 0, off, width)

    def step(i, carry):
        slot = lax.rem(i, 2)
        for off, width in tiles():
            logits_tile(e_ref, c_ref, buf, i + 1, 1 - slot, off, width)
            label_tile(lse_ref, m_ref, buf, acc, i, slot, off, width)
        return carry

    lax.fori_loop(0, CHUNKS - 1, step, 0)
    column = lax.axis_index("cls") * N
    for off, width in tiles():
        label_tile(lse_ref, m_ref, buf, acc, CHUNKS - 1, (CHUNKS - 1) % 2, off, width)
        here = column + off + lax.broadcasted_iota(jnp.int32, (ROWS, width), 1)
        o_ref[:, off : off + width] = jnp.where(here < LIVE, acc[:, off : off + width], 0.0)


def shards(embeddings, class_text_embedding, neighbours, weights, requests):
    me = lax.axis_index("img")
    live = (lax.axis_index("cls") * N + jnp.arange(N) < LIVE)[None, :]
    offset = neighbours - ROWS
    hot = jnp.maximum(offset, 0)[:, :, None] == jnp.arange(PEERS * CAP)
    asked = jnp.sum(jnp.where(hot, requests.reshape(PEERS * CAP), 0), axis=2)
    peer = jnp.where(offset >= 0, jnp.maximum(offset, 0) // CAP, me)
    row = jnp.where(offset >= 0, asked, neighbours)
    scale = 1.0 / (1.0 + jnp.sum(weights, axis=1, keepdims=True))
    value_hi, value_lo = split(jnp.concatenate([scale, weights * scale], axis=1))
    own_row = jnp.arange(ROWS, dtype=jnp.int32)[:, None]
    peers = jnp.concatenate([jnp.full((ROWS, 1), me, jnp.int32), peer], axis=1).astype(BF16)
    rows = jnp.concatenate([own_row, row], axis=1).astype(BF16)
    gap = jnp.zeros((ROWS, 16 - (K + 1)), BF16)
    table = jnp.concatenate([peers, gap, rows, gap, value_hi, gap, value_lo, gap, jnp.zeros((ROWS, 64), BF16)], axis=1)
    extended = lax.all_gather(jnp.concatenate([embeddings, table], axis=1), "img", axis=0, tiled=True)

    logits = jnp.where(live, dot(embeddings, class_text_embedding), -1e30)
    top = lax.pmax(jnp.max(logits, axis=1), "cls")
    total = lax.psum(jnp.sum(jnp.where(live, jnp.exp(logits - top[:, None]), 0.0), axis=1), "cls")
    lse = lax.all_gather(top + jnp.log(total), "img", axis=0, tiled=True)
    lse = jnp.broadcast_to(lse[:, None], (ALL, 128))

    vmem = pl.BlockSpec(memory_space=pltpu.VMEM)
    return pl.pallas_call(
        kernel,
        out_shape=jax.ShapeDtypeStruct((ROWS, N), F32),
        in_specs=[vmem] * 6,
        out_specs=vmem,
        scratch_shapes=[
            pltpu.VMEM((2, CHUNK, N), F32),
            pltpu.VMEM((ROWS, N), F32),
            pltpu.VMEM((K * ROWS, 128), F32),
            pltpu.VMEM((ROWS, 128), jnp.int32),
            pltpu.VMEM((ROWS, 128), jnp.int32),
            pltpu.VMEM((ROWS, 128), F32),
            pltpu.VMEM((24 * ROWS, 128), F32),
            pltpu.VMEM((CHUNKS, 2 * ROWS, CHUNK), BF16),
        ],
        compiler_params=pltpu.CompilerParams(vmem_limit_bytes=56 << 20),
    )(extended, class_text_embedding, lse, peer, row, weights)


def solution(mesh):
    in_specs = (
        P("img", None),
        P(None, "cls"),
        P("img", None),
        P("img", None),
        P("img", None, None),
    )
    return jax.shard_map(shards, mesh=mesh, in_specs=in_specs, out_specs=P("img", "cls"), check_vma=False)
```

time: 468 us -> 291 us (0.62)
  the two profiles are of different devices: /device:TPU:1 before, /device:TPU:0 now
where the time goes in v1:
time: 291 us
  blocking collectives  172 us (59%)
  Pallas kernels  81.1 us (28%)
  local copies, waits for them, and re-layouts  15.4 us (5%)
  between operations  14.2 us (5%)
  matrix products  4.51 us (2%)
  other arithmetic  3.16 us (1%)
    unnamed x1, blocking collectives  147 us
    pallas_call x1, Pallas kernels, shards(): pl.pallas_call(kernel, out_shape=jax.ShapeDtypeStruct((ROWS, N), F32), in...  81.1 us
    pmax x1, blocking collectives, shards(): top = lax.pmax(jnp.max(logits, axis=1), 'cls')  13.3 us
    psum x1, blocking collectives, shards(): lax.psum(jnp.sum(jnp.where(live, jnp.exp(logits - top[:, None]), 0.0), ax...  12.5 us
    unnamed x12, local copies, waits for them, and re-layouts  11.3 us
  transfers between devices with their start and end apart: 1, of which 0 were waited for; matrix products, arithmetic and copies ran while one was open for 5% of the time, Pallas kernels for 0%

profile of v1, /device:TPU:0, one launch (start us, length us, event | category | flops | bytes accessed | tf_op | source)
XLA Modules:
  0.0 290.8 jit_solution(2129633614589130660)
XLA Ops:
  6.5 0.0 copy-start.1
  6.5 0.0 all-gather.2.cloned.1.call-start
  6.5 0.8 reduce_sum.28
  7.4 0.7 broadcast_multiply_fusion
  8.1 0.1 copy.44
  8.2 0.1 copy.43
  8.3 0.8 copy.39
  9.1 0.1 reshape.27
  9.2 0.1 copy.42
  9.3 0.8 copy.37
  10.1 0.1 copy.38
  10.1 0.5 select_reduce_fusion
  10.6 0.1 copy.40
  10.7 0.7 fusion.4
  11.4 0.1 concatenate.12
  11.5 1.8 concatenate.14
  13.3 0.0 all-gather.2.cloned.1.call-update
  13.3 0.0 copy-done.1
  13.3 0.7 copy.46.w_ref
  14.0 0.0 copy-start
  14.0 8.4 %copy.45.c_ref = bf16[1024,2736]{1,0:T(8,128)(2,1)} copy(bf16[1024,2736]{0,1:T(8,128)(2,1)} %param.6) | data formatting | bytes 11206656 | tf_op args[1]
  22.4 0.0 copy-done.2
  22.4 0.7 dynamic-slice
  23.8 0.0 copy-done
  23.8 4.5 %fusion.8 = (f32[96]{0:T(128)S(1)}, f32[96,2736]{1,0:T(8,128)S(1)}) fusion(bf16[96,1024]{1,0:T(8,128)(2,1)S(1)} %copy-done, bf16[1024,2736]{0,1:T(8,128)(2,1)} %param.6, pred[2736]{0:T(1024)(128)(4,1)S(1)} %add_compare_fusion.1), kind=kOutput, calls=%fused_computation.22 | convolution fusion | flops 538444672 | bytes 6853680 | tf_op jit(solution)/shard_map/dot_general | solution.py:26
  28.3 13.3 %pmax.7 = f32[96]{0:T(128)S(1)} all-reduce(f32[96]{0:T(128)S(1)} %get-tuple-element.13), channel_id=1, replica_groups=mesh['img'=32,'cls'=8] {'cls'}, use_global_device_ids=true, to_apply=%region_3.4 | all-reduce | flops 96 | bytes 768 | tf_op jit(solution)/shard_map/pmax | solution.py:150
  41.6 0.4 select_reduce_fusion.1
  42.0 12.5 %psum.7 = f32[96]{0:T(128)S(1)} all-reduce(f32[96]{0:T(128)S(1)} %select_reduce_fusion.1), channel_id=1, replica_groups=mesh['img'=32,'cls'=8] {'cls'}, use_global_device_ids=true, to_apply=%region_5.6 | all-reduce | flops 96 | bytes 768 | tf_op jit(solution)/shard_map/psum | solution.py:151
  54.5 0.1 add_dynamic-update-slice_fusion
  54.7 146.5 %all-reduce.1 = f32[3072]{0:T(1024)S(1)} all-reduce(f32[3072]{0:T(1024)S(1)} %add_dynamic-update-slice_fusion), channel_id=1, replica_groups=mesh['img'=32,'cls'=8] {'img'}, use_global_device_ids=true, to_apply=%add.1 | all-reduce | flops 3072 | bytes 24576
  201.2 1.6 broadcast_in_dim.57.lse_ref
  202.8 81.1 %shard_map.55 = f32[96,2736]{1,0:T(8,128)} custom-call(bf16[3072,1152]{1,0:T(8,128)(2,1)} %all-gather.2.cloned.1.call-done.e_ref, bf16[1024,2736]{1,0:T(8,128)(2,1)} %copy.45.c_ref, f32[3072,128]{1,0:T(8,128)} %broadcast_in_dim.57.lse_ref, s32[96,10]{1,0:T(8,128)} %get-tuple-element.12.peer_ref, s32[96,10]{1,0:T(8,128)} %get-tuple-element.8.row_ref, ...), custom_call_target="tpu_custom_call" | custom-call | tf_op jit(solution)/shard_map/pallas_call | solution.py:156
  (12 shorter events, 0.1 us)
Async XLA Ops:
  6.5 6.8 %copy-start.1 = (f32[96,10]{0,1:T(8,128)S(1)}, f32[96,10]{0,1:T(8,128)}, u32[]{:S(2)}) copy-start(f32[96,10]{0,1:T(8,128)} %param.8) | copy-start | bytes 11524
  6.5 194.6 %all-gather.2.cloned.1.call-start = ((), (), s32[]{:S(2)}) async-start(), calls=%async_computation | async-start | bytes 7299072 | tf_op jit(solution)/shard_map/all_gather | solution.py:147
  14.0 8.4 %copy-start.2 = (u32[256]{0:T(256)S(1)}, u32[256]{0:T(256)}, u32[]{:S(2)}) copy-start(u32[256]{0:T(256)} %constant.52) | copy-start | bytes 3076
  14.0 9.7 %copy-start = (bf16[96,1024]{1,0:T(8,128)(2,1)S(1)}, bf16[96,1024]{1,0:T(8,128)(2,1)}, u32[]{:S(2)}) copy-start(bf16[96,1024]{1,0:T(8,128)(2,1)} %param.5) | copy-start | bytes 589828
Sparse Core Ops, SparseCore 0:
  13.4 94.0 all-gather.1

commit v2 on v0

v2 whole, which is shorter than its diff:
```python
import jax
import jax.numpy as jnp
from jax import lax
from jax.experimental import pallas as pl
from jax.experimental.pallas import tpu as pltpu
from jax.sharding import PartitionSpec as P

LIVE = 21841
ROWS = 96
HALF = 48
K = 10
PEERS = 32
CLS = 8
ALL = ROWS * PEERS
D = 1024
N = 2736
TN = 256
CHUNK = 512
CHUNKS = ALL // CHUNK
PACK = 32
F32 = jnp.float32
BF16 = jnp.bfloat16
MESH = pl.DeviceIdType.MESH
TILES = [(off, min(TN, N - off)) for off in range(0, N, TN)]
B_BASE = (0, 1536, 2048, 2560)
A_BASE = 512
MESSAGES = 40


def dot(a, b):
    return jnp.dot(a, b, preferred_element_type=F32)


def dot_nt(a, b):
    return lax.dot_general(a, b, (((1,), (1,)), ((), ())), preferred_element_type=F32)


def split(x):
    hi = x.astype(BF16)
    return hi, (x - hi.astype(F32)).astype(BF16)


def iota(shape, axis):
    return lax.broadcasted_iota(jnp.int32, shape, axis)


def relative(z, y, peer):
    return ((peer >> 2) - z) & 7, ((peer & 3) - y) & 3


def place(z, y, peer, row):
    dz, dy = relative(z, y, peer)
    zi = jnp.where(dz == 0, 0, jnp.where(dz <= 4, 2 * dz - 1, 16 - 2 * dz))
    yi = jnp.where(dy < 2, dy, 5 - dy)
    half = jnp.where(row >= HALF, 1, 0)
    t = row - HALF * half
    in_a = A_BASE + half * 512 + zi * 64 + yi * 16 + t
    in_b = jnp.where(yi == 0, 0, 1024 + 512 * yi) + half * 256 + zi * 32 + t - 16
    return jnp.where(t < 16, in_a, in_b)


def kernel(
    e_ref, ct_hbm, near_ref, w_ref, ask_ref, o_ref,
    every, ct, buf0, buf1, acc, lse_ref, m_ref, dense, table, all_tables, own, xs, ys, lists_a, lists_b, lists_v, got, stats, lses,
    ct_sem, ssem, rsem, table_sem, stat_sem, lse_sem, m_sem,
):
    me, c = lax.axis_index("img"), lax.axis_index("cls")
    z, y, h = me // 4, lax.rem(me, 4), lax.rem(c, 2)
    bufs = (buf0, buf1)

    load_ct = pltpu.make_async_copy(ct_hbm, ct, ct_sem)
    load_ct.start()

    barrier = pltpu.get_barrier_semaphore()

    def greet_img(j, carry):
        pl.semaphore_signal(barrier, inc=1, device_id={"img": lax.rem(me + j, PEERS)}, device_id_type=MESH)
        return carry

    def greet_cls(j, carry):
        pl.semaphore_signal(barrier, inc=1, device_id={"cls": lax.rem(c + j, CLS)}, device_id_type=MESH)
        return carry

    lax.fori_loop(1, PEERS, greet_img, 0)
    lax.fori_loop(1, CLS, greet_cls, 0)

    for half in range(2):
        every[A_BASE + 512 * half : A_BASE + 512 * half + 16, :] = e_ref[HALF * half : HALF * half + 16, :]
        every[256 * half : 256 * half + 32, :] = e_ref[HALF * half + 16 : HALF * half + HALF, :]

    near = near_ref[...]
    w_t = w_ref[...]
    far = jnp.maximum(near - ROWS, 0)
    source, within = far >> 4, far & 15
    asks = ask_ref[...].astype(F32).astype(BF16)
    ys[...] = jnp.zeros_like(ys)
    ys[0:K, 0:ROWS] = jnp.where(near >= ROWS, source, me).astype(F32)
    for k in range(K):
        hot = jnp.where(iota((PEERS, ROWS), 0) == source[k : k + 1, :], 1.0, 0.0).astype(BF16)
        picked = dot(asks, hot)
        asked = jnp.sum(jnp.where(iota((16, ROWS), 0) == within[k : k + 1, :], picked, 0.0), axis=0, keepdims=True)
        ys[16 + k : 17 + k, 0:ROWS] = jnp.where(near[k : k + 1, :] >= ROWS, asked, near[k : k + 1, :].astype(F32))
    ys[32 : 32 + K, 0:ROWS] = w_t
    w_hi = w_t.astype(BF16).astype(F32)
    pieces = [ys[0:K, 0:ROWS], ys[16 : 16 + K, 0:ROWS], w_hi, w_t - w_hi]
    xs[...] = jnp.zeros_like(xs)
    for q in range(3):
        for i, piece in enumerate(pieces):
            at = q * 4 * K + i * K
            xs[at : at + K, 0:PACK] = piece[:, q * PACK : (q + 1) * PACK]
    table[...] = xs[...].T[:PACK, :].astype(BF16)
    all_tables[0:PACK, :] = table[...]
    own[...] = ys[...].T

    pl.semaphore_wait(barrier, PEERS - 1 + CLS - 1)

    def peer_at(j):
        return {"img": lax.rem(z + 8 - j // 4, 8) * 4 + lax.rem(y + 4 - lax.rem(j, 4), 4)}

    def table_copy(j, n):
        rows = pl.ds(pl.multiple_of(j * PACK, PACK), n * PACK)
        src = table if n == 1 else all_tables.at[rows]
        return pltpu.make_async_remote_copy(src, all_tables.at[rows], table_sem.at[0], table_sem.at[1], device_id=peer_at(j), device_id_type=MESH)

    def send_table(j, carry):
        table_copy(j, 1).start()
        return carry

    lax.fori_loop(1, PEERS, send_table, 0)

    y_up, y_down = {"img": z * 4 + lax.rem(y + 1, 4)}, {"img": z * 4 + lax.rem(y + 3, 4)}
    z_up, z_down = {"img": lax.rem(z + 1, 8) * 4 + y}, {"img": lax.rem(z + 7, 8) * 4 + y}
    sibling = {"cls": c + 1 - 2 * h}
    made = {}

    def go(name, src, dst, n, target, columns=slice(None)):
        i = len(made)
        src = pl.ds(pl.multiple_of(src, 16), n)
        dst = pl.ds(pl.multiple_of(dst, 16), n)
        copy = pltpu.make_async_remote_copy(
            every.at[src, columns], every.at[dst, columns], ssem.at[i], rsem.at[i], device_id=target, device_id_type=MESH
        )
        copy.start()
        made[name] = copy

    def take(*names):
        for name in names:
            made[name].wait_recv()

    def at_a(zi, yi=0):
        return A_BASE + 512 * h + 64 * zi + 16 * yi

    def at_b(yi, zi=0):
        return B_BASE[yi] + 256 * h + 32 * zi

    def share(name, at, n):
        go(name, at, at, n, sibling)

    def round_0():
        go("a_y2", at_a(0), at_a(0, 2), 16, y_up)
        go("a_y1", at_a(0), at_a(0, 1), 16, y_down)
        go("b_z2", at_b(0), at_b(0, 2), 32, z_up)
        go("b_z1", at_b(0), at_b(0, 1), 32, z_down)

    def round_1():
        take("a_y1", "a_y2", "b_z1", "b_z2")
        go("a_y3u", at_a(0, 2), at_a(0, 3), 16, y_up, slice(0, 512))
        go("a_y3d", at_a(0, 1), at_a(0, 3), 16, y_down, slice(512, 1024))
        go("b_z4", at_b(0, 2), at_b(0, 4), 32, z_up)
        go("b_z3", at_b(0, 1), at_b(0, 3), 32, z_down)
        go("b_y2q0", at_b(0), at_b(2), 96, y_up)
        go("b_y1q0", at_b(0), at_b(1), 96, y_down)

    def round_2():
        take("a_y3u", "a_y3d", "b_z3", "b_z4")
        go("a_z2", at_a(0), at_a(2), 64, z_up)
        go("a_z1", at_a(0), at_a(1), 64, z_down)
        go("b_z6", at_b(0, 4), at_b(0, 6), 32, z_up)
        go("b_z5", at_b(0, 3), at_b(0, 5), 32, z_down)
        share("a_s0", at_a(0, 1), 48)

    def round_3():
        take("b_z5", "b_z6")
        go("b_z7u", at_b(0, 6), at_b(0, 7), 16, z_up)
        go("b_z7d", at_b(0, 5) + 16, at_b(0, 7) + 16, 16, z_down)
        take("a_z1", "a_z2")
        go("a_z4", at_a(2), at_a(4), 64, z_up)
        go("a_z3", at_a(1), at_a(3), 64, z_down)
        share("a_s1", at_a(1), 128)

    def round_4():
        take("b_z7u", "b_z7d")
        go("b_y2q1", at_b(0, 3), at_b(2, 3), 160, y_up)
        go("b_y1q1", at_b(0, 3), at_b(1, 3), 160, y_down)
        share("b_s0", at_b(0, 1), 224)
        take("a_z3", "a_z4")
        go("a_z6", at_a(4), at_a(6), 64, z_up)
        go("a_z5", at_a(3), at_a(5), 64, z_down)
        share("a_s3", at_a(3), 128)

    def round_5():
        take("b_y1q0", "b_y2q0")
        go("b_y3q0u", at_b(2), at_b(3), 48, y_up)
        go("b_y3q0d", at_b(1) + 48, at_b(3) + 48, 48, y_down)
        take("a_z5", "a_z6")
        go("a_z7u", at_a(6), at_a(7), 32, z_up)
        go("a_z7d", at_a(5) + 32, at_a(7) + 32, 32, z_down)

    def round_6():
        take("a_z7u", "a_z7d")
        share("a_s5", at_a(5), 192)

    def round_7():
        take("b_y1q1", "b_y2q1")
        go("b_y3q1u", at_b(2, 3), at_b(3, 3), 80, y_up)
        go("b_y3q1d", at_b(1, 3) + 80, at_b(3, 3) + 80, 80, y_down)
        share("b_s1", at_b(1), 256)
        share("b_s2", at_b(2), 256)

    def round_8():
        take("b_y3q0u", "b_y3q0d", "b_y3q1u", "b_y3q1d")
        share("b_s3", at_b(3), 256)

    round_0()

    load_ct.wait()
    column = c * N
    top = jnp.full((ROWS, 1), -1e30, F32)
    for off, width in TILES:
        logits = dot_nt(e_ref[...], ct[off : off + width, :])
        logits = jnp.where(column + off + iota((ROWS, width), 1) < LIVE, logits, -1e30)
        buf1[0:ROWS, off : off + width] = logits
        top = jnp.maximum(top, jnp.max(logits, axis=1, keepdims=True))
    round_1()
    total = jnp.zeros((ROWS, 1), F32)
    for off, width in TILES:
        total += jnp.sum(jnp.exp(buf1[0:ROWS, off : off + width] - top), axis=1, keepdims=True)
    lanes = iota((ROWS, 128), 1)
    xs[...] = jnp.zeros_like(xs)
    xs[0:ROWS, :] = jnp.where(lanes == 0, top, jnp.where(lanes == 1, total, 0.0))
    stats[0] = xs[...].T[:8, :]

    def stat_copy(j, n):
        src = stats.at[0] if n == 1 else stats.at[pl.ds(j, n)]
        dst = stats.at[j] if n == 1 else stats.at[pl.ds(j, n)]
        return pltpu.make_async_remote_copy(
            src, dst, stat_sem.at[0], stat_sem.at[1], device_id={"cls": lax.rem(c + j, CLS)}, device_id_type=MESH
        )

    def send_stat(j, carry):
        stat_copy(j, 1).start()
        return carry

    lax.fori_loop(1, CLS, send_stat, 0)
    round_2()

    table_copy(1, PEERS - 1).wait_recv()
    mine = own[pl.ds(pl.multiple_of(HALF * h, 16), HALF), :]
    lanes = iota((HALF, 128), 1)
    peer = mine.astype(jnp.int32)
    row = pltpu.roll(mine, 128 - 16, 1).astype(jnp.int32)
    weight = pltpu.roll(mine, 128 - 32, 1)
    scale = 1.0 / (1.0 + jnp.sum(jnp.where(lanes < K, weight, 0.0), axis=1, keepdims=True))
    dz, dy = relative(z, y, peer)
    packed = (dz * 4 + dy) * PACK + (row & (PACK - 1))
    group = row >> 5
    for step in range(4):
        at = iota((HALF, 256), 1) + step * 256
        hot = [jnp.where(at == packed[:, k : k + 1], 1.0, 0.0).astype(BF16) for k in range(K)]
        part = dot(jnp.concatenate(hot, axis=0), all_tables[step * 256 : step * 256 + 256, :])
        got[...] = part if step == 0 else got[...] + part
    peers = jnp.zeros((HALF, 128), F32)
    rows = jnp.zeros((HALF, 128), F32)
    values = jnp.zeros((HALF, 128), F32)
    for k in range(K):
        g = got[k * HALF : (k + 1) * HALF, :]
        q = group[:, k : k + 1]
        g = jnp.where(q == 0, g, jnp.where(q == 1, pltpu.roll(g, 128 - 4 * K, 1), pltpu.roll(g, 128 - 8 * K, 1)))
        edge = jnp.where(lanes < K, pltpu.roll(g, 128 - 2 * K, 1) + pltpu.roll(g, 128 - 3 * K, 1), 0.0)
        outer = weight[:, k : k + 1] / (1.0 + jnp.sum(edge, axis=1, keepdims=True))
        self_lane = lanes == K
        pk = jnp.where(self_lane, peer[:, k : k + 1].astype(F32), jnp.where(lanes < K, g, 0.0))
        rk = jnp.where(self_lane, row[:, k : k + 1].astype(F32), jnp.where(lanes < K, pltpu.roll(g, 128 - K, 1), 0.0))
        vk = jnp.where(self_lane, outer, edge * outer)
        if k:
            pk, rk, vk = pltpu.roll(pk, 12 * k, 1), pltpu.roll(rk, 12 * k, 1), pltpu.roll(vk, 12 * k, 1)
        peers, rows, values = peers + pk, rows + rk, values + vk
    itself = lanes == 12 * K
    peers = jnp.where(itself, me, peers.astype(jnp.int32))
    rows = jnp.where(itself, HALF * h + iota((HALF, 128), 0), rows.astype(jnp.int32))
    where = place(z, y, peers, rows)
    lists_a[...] = where >> 7
    lists_b[...] = where & 127
    lists_v[...] = jnp.where(itself, 1.0, values) * scale
    round_3()

    stat_copy(1, CLS - 1).wait_recv()
    top = stats[0, 0:1, :]
    for j in range(1, CLS):
        top = jnp.maximum(top, stats[j, 0:1, :])
    total = jnp.zeros((1, 128), F32)
    for j in range(CLS):
        total += stats[j, 1:2, :] * jnp.exp(stats[j, 0:1, :] - top)
    lses[0] = top + jnp.log(total)

    def lse_copy(j, n):
        src = lses.at[0] if n == 1 else lses.at[pl.ds(j, n)]
        dst = lses.at[j] if n == 1 else lses.at[pl.ds(j, n)]
        return pltpu.make_async_remote_copy(src, dst, lse_sem.at[0], lse_sem.at[1], device_id=peer_at(j), device_id_type=MESH)

    def send_lse(j, carry):
        lse_copy(j, 1).start()
        return carry

    lax.fori_loop(1, PEERS, send_lse, 0)

    def scatter(r, carry):
        a, b, v = lists_a[pl.ds(r, 1), :], lists_b[pl.ds(r, 1), :], lists_v[pl.ds(r, 1), :]
        left = jnp.where(iota((32, 128), 0) == a, v, 0.0)
        right = jnp.where(iota((128, 128), 0) == b, 1.0, 0.0).astype(BF16)
        out = dot_nt(jnp.concatenate(split(left), axis=0), right)
        dense[pl.ds(r, 24, stride=HALF), :] = out[:24] + out[32:56]
        return carry

    lax.fori_loop(0, HALF, scatter, 0, unroll=8)
    per = CHUNK // 128
    mine_hi = pl.ds(pl.multiple_of(HALF * h, 16), HALF)
    mine_lo = pl.ds(pl.multiple_of(HALF * h + ROWS, 16), HALF)
    for i in range(CHUNKS):
        block = jnp.concatenate([dense[(per * i + j) * HALF : (per * i + j + 1) * HALF, :] for j in range(per)], axis=1)
        hi, lo = split(block)
        m_ref[i, mine_hi, :] = hi
        m_ref[i, mine_lo, :] = lo
    m_copies = [
        pltpu.make_async_remote_copy(
            m_ref.at[:, part, :], m_ref.at[:, part, :], m_sem.at[i, 0], m_sem.at[i, 1], device_id=sibling, device_id_type=MESH
        )
        for i, part in enumerate((mine_hi, mine_lo))
    ]
    for copy in m_copies:
        copy.start()
    round_4()

    lse_copy(1, PEERS - 1).wait_recv()
    xs[...] = jnp.zeros_like(xs)
    xs[0:PEERS, :] = lses[:, 0, :]
    ys[...] = xs[...].T
    for dz in range(8):
        for dy in range(4):
            zi = 0 if dz == 0 else 2 * dz - 1 if dz <= 4 else 16 - 2 * dz
            yi = dy if dy < 2 else 5 - dy
            for half in range(2):
                col = jnp.broadcast_to(ys[HALF * half : HALF * half + HALF, dz * 4 + dy : dz * 4 + dy + 1], (HALF, 128))
                a = A_BASE + 512 * half + 64 * zi + 16 * yi
                b = B_BASE[yi] + 256 * half + 32 * zi
                lse_ref[a : a + 16, :] = col[:16]
                lse_ref[b : b + 32, :] = col[16:]
    acc[...] = jnp.zeros_like(acc)
    round_5()
    take("b_s0")

    def logits_tile(chunk, off, width):
        bufs[chunk % 2][:, off : off + width] = dot_nt(every[chunk * CHUNK : (chunk + 1) * CHUNK, :], ct[off : off + width, :])

    def label_tile(chunk, off, width):
        lse = lse_ref[chunk * CHUNK : (chunk + 1) * CHUNK, :]
        lse = jnp.concatenate([lse] * (-(-width // 128)), axis=1)[:, :width]
        hi, lo = split(jnp.exp(bufs[chunk % 2][:, off : off + width] - lse))
        m = m_ref[chunk]
        a = dot(m, hi)
        acc[:, off : off + width] += a[:ROWS] + a[ROWS:] + dot(m[:ROWS], lo)

    for off, width in TILES:
        logits_tile(0, off, width)
    for copy in m_copies:
        copy.wait_recv()
    round_6()
    take("a_s0", "a_s1", "a_s3", "a_s5")
    before = {0: [], 1: [round_7], 2: [round_8, lambda: take("b_s1")], 3: [lambda: take("b_s2")], 4: [lambda: take("b_s3")]}
    for chunk in range(CHUNKS):
        for event in before.get(chunk, []):
            event()
        for off, width in TILES:
            if chunk + 1 < CHUNKS:
                logits_tile(chunk + 1, off, width)
            label_tile(chunk, off, width)
    for off, width in TILES:
        here = column + off + iota((ROWS, width), 1)
        o_ref[:, off : off + width] = jnp.where(here < LIVE, acc[:, off : off + width], 0.0)

    for copy in made.values():
        copy.wait_send()
    for copy in m_copies:
        copy.wait_send()
    table_copy(1, PEERS - 1).wait_send()
    stat_copy(1, CLS - 1).wait_send()
    lse_copy(1, PEERS - 1).wait_send()


def shards(embeddings, class_text_embedding, neighbours, weights, requests):
    vmem = pl.BlockSpec(memory_space=pltpu.VMEM)
    dma = pltpu.SemaphoreType.DMA
    return pl.pallas_call(
        kernel,
        out_shape=jax.ShapeDtypeStruct((ROWS, N), F32),
        in_specs=[vmem, pl.BlockSpec(memory_space=pl.ANY), vmem, vmem, vmem],
        out_specs=vmem,
        scratch_shapes=[
            pltpu.VMEM((ALL, D), BF16),
            pltpu.VMEM((N, D), BF16),
            pltpu.VMEM((CHUNK, N), F32),
            pltpu.VMEM((CHUNK, N), F32),
            pltpu.VMEM((ROWS, N), F32),
            pltpu.VMEM((ALL, 128), F32),
            pltpu.VMEM((CHUNKS, 2 * ROWS, CHUNK), BF16),
            pltpu.VMEM((24 * HALF, 128), F32),
            pltpu.VMEM((PACK, 128), BF16),
            pltpu.VMEM((PEERS * PACK, 128), BF16),
            pltpu.VMEM((128, 128), F32),
            pltpu.VMEM((128, 128), F32),
            pltpu.VMEM((128, 128), F32),
            pltpu.VMEM((HALF, 128), jnp.int32),
            pltpu.VMEM((HALF, 128), jnp.int32),
            pltpu.VMEM((HALF, 128), F32),
            pltpu.VMEM((K * HALF, 128), F32),
            pltpu.VMEM((CLS, 8, 128), F32),
            pltpu.VMEM((PEERS, 1, 128), F32),
            dma,
            dma((MESSAGES,)),
            dma((MESSAGES,)),
            dma((2,)),
            dma((2,)),
            dma((2,)),
            dma((2, 2)),
        ],
        compiler_params=pltpu.CompilerParams(vmem_limit_bytes=56 << 20, collective_id=0, has_side_effects=True),
    )(embeddings, class_text_embedding.T, neighbours.T, weights.T, requests[0].T)


def solution(mesh):
    in_specs = (
        P("img", None),
        P(None, "cls"),
        P("img", None),
        P("img", None),
        P("img", None, None),
    )
    return jax.shard_map(shards, mesh=mesh, in_specs=in_specs, out_specs=P("img", "cls"), check_vma=False)
```

time: 468 us -> 75.1 us (0.16)
  blocking collectives: 168 us -> 0 us
  waiting for transfers between devices: 126 us -> 0 us
  local copies, waits for them, and re-layouts: 115 us -> 2.29 us
  Pallas kernels: 0 us -> 72.6 us
  other arithmetic: 29.4 us -> 0 us
  starting transfers between devices: 21.5 us -> 0 us
    all_to_all x1 -> x0, blocking collectives: 141 us -> none  [shards(): lax.all_to_all(outgoing(second), 'img', split_axis=0, concat_axis=0, tile...]
    all_to_all x2 -> x0, waiting for transfers between devices: 126 us -> none  [the longest x1 126 us: shards(): lax.all_to_all(outgoing(first), 'img', split_axis=0, concat_axis=0, tiled...]
    gather x22 -> x0, local copies, waits for them, and re-layouts: 113 us -> none  [the longest x20 104 us: sweep(): acc = acc + weights[:, k:k + 1] * extended[neighbours[:, k]]]
    pallas_call x0 -> x1, Pallas kernels: none -> 72.6 us  [shards(): pl.pallas_call(kernel, out_shape=jax.ShapeDtypeStruct((ROWS, N), F32), in...]
    all_to_all x2 -> x0, starting transfers between devices: 21.5 us -> none  [the longest x1 12 us: shards(): lax.all_to_all(requests[0], 'img', split_axis=0, concat_axis=0, tiled=True)]
    psum x1 -> x0, blocking collectives: 14.5 us -> none  [probabilities(): total = lax.psum(jnp.sum(powers, axis=1), 'cls')]
    pmax x1 -> x0, blocking collectives: 12.7 us -> none  [probabilities(): top = lax.pmax(local_top, 'cls')]
    div x3 -> x0, other arithmetic: 11.2 us -> none  [the longest x2 11 us: sweep(): return (first + smoothing * acc) / (1.0 + smoothing * degree)]
  transfers between devices with their start and end apart: 2 -> 0, of which waited for: 1 -> 0; matrix products, arithmetic and copies ran while one was open for 1% -> 0% of each run, Pallas kernels for 0% -> 0%
where the time goes in v2:
time: 75.1 us; the launch traced here: 74.9 us
  Pallas kernels  72.6 us (97%)
  local copies, waits for them, and re-layouts  2.29 us (3%)
    pallas_call x1, Pallas kernels, shards(): pl.pallas_call(kernel, out_shape=jax.ShapeDtypeStruct((ROWS, N), F32), in...  72.6 us
    unnamed x1, local copies, waits for them, and re-layouts  2.29 us

profile of v2, /device:TPU:1, one launch (start us, length us, event | category | flops | bytes accessed | tf_op | source)
XLA Modules:
  0.0 74.9 jit_solution(15795372533143873015)
XLA Ops:
  0.0 72.6 %shard_map.55 = f32[96,2736]{1,0:T(8,128)} custom-call(bf16[96,1024]{1,0:T(8,128)(2,1)} %e_ref.1, bf16[2736,1024]{1,0:T(8,128)(2,1)} %bitcast.6, s32[10,96]{1,0:T(8,128)} %bitcast.7, f32[10,96]{1,0:T(8,128)} %bitcast.8, s32[16,32]{1,0:T(8,128)} %bitcast.9), custom_call_target="tpu_custom_call" | custom-call | tf_op jit(solution)/shard_map/pallas_call | solution.py:403
  72.6 2.3 %copy.7 = f32[96,2736]{1,0:T(8,128)} copy(f32[96,2736]{1,0:T(8,128)} %shard_map.55) | data formatting | bytes 2101248

commit v3 on v2

--- a/solution.py
+++ b/solution.py
@@ -15,16 +15,22 @@
 D = 1024
 N = 2736
 TN = 256
-CHUNK = 512
-CHUNKS = ALL // CHUNK
 PACK = 32
 F32 = jnp.float32
 BF16 = jnp.bfloat16
 MESH = pl.DeviceIdType.MESH
 TILES = [(off, min(TN, N - off)) for off in range(0, N, TN)]
-B_BASE = (0, 1536, 2048, 2560)
-A_BASE = 512
-MESSAGES = 40
+A_AT = [(0, 1152)] + [(s + 64 * i, 128) for s in (512, 1280, 1792) for i in range(2)] + [(2304, 64)]
+B_AT = [
+    [(64 + 32 * i, 224) for i in range(7)] + [(1216, 32)],
+    [(768 + 32 * i, 96) for i in range(3)] + [(s + 32 * i, 64) for s in (1536, 2048) for i in range(2)] + [(2432, 32)],
+    [(960 + 32 * i, 96) for i in range(3)] + [(s + 32 * i, 64) for s in (1664, 2176) for i in range(2)] + [(2496, 32)],
+    [(2816 + 32 * i, 96) for i in range(3)] + [(2560 + 32 * i, 128) for i in range(4)] + [(3008, 32)],
+]
+CHUNK_AT = (0, 512, 1152, 1792, 2304, 2816, 3072)
+CHUNKS = 6
+CHUNK = 640
+MESSAGES = 72
 
 
 def dot(a, b):
@@ -54,9 +60,12 @@
     yi = jnp.where(dy < 2, dy, 5 - dy)
     half = jnp.where(row >= HALF, 1, 0)
     t = row - HALF * half
-    in_a = A_BASE + half * 512 + zi * 64 + yi * 16 + t
-    in_b = jnp.where(yi == 0, 0, 1024 + 512 * yi) + half * 256 + zi * 32 + t - 16
-    return jnp.where(t < 16, in_a, in_b)
+    a, b = jnp.zeros_like(t), jnp.zeros_like(t)
+    for i in range(8):
+        a = jnp.where(zi == i, A_AT[i][0] + A_AT[i][1] * half, a)
+        for j in range(4):
+            b = jnp.where(jnp.logical_and(zi == i, yi == j), B_AT[j][i][0] + B_AT[j][i][1] * half, b)
+    return jnp.where(t < 16, a + 16 * yi + t, b + t - 16)
 
 
 def kernel(
@@ -85,8 +94,9 @@
     lax.fori_loop(1, CLS, greet_cls, 0)
 
     for half in range(2):
-        every[A_BASE + 512 * half : A_BASE + 512 * half + 16, :] = e_ref[HALF * half : HALF * half + 16, :]
-        every[256 * half : 256 * half + 32, :] = e_ref[HALF * half + 16 : HALF * half + HALF, :]
+        a, b = A_AT[0][0] + A_AT[0][1] * half, B_AT[0][0][0] + B_AT[0][0][1] * half
+        every[a : a + 16, :] = e_ref[HALF * half : HALF * half + 16, :]
+        every[b : b + 32, :] = e_ref[HALF * half + 16 : HALF * half + HALF, :]
 
     near = near_ref[...]
     w_t = w_ref[...]
@@ -112,6 +122,24 @@
     all_tables[0:PACK, :] = table[...]
     own[...] = ys[...].T
 
+    load_ct.wait()
+    column = c * N
+    top = jnp.full((ROWS, 1), -1e30, F32)
+    for off, width in TILES:
+        logits = dot_nt(e_ref[...], ct[off : off + width, :])
+        logits = jnp.where(column + off + iota((ROWS, width), 1) < LIVE, logits, -1e30)
+        buf1[0:ROWS, off : off + width] = logits
+        top = jnp.maximum(top, jnp.max(logits, axis=1, keepdims=True))
+    total = jnp.zeros((ROWS, 1), F32)
+    for off, width in TILES:
+        total += jnp.sum(jnp.exp(buf1[0:ROWS, off : off + width] - top), axis=1, keepdims=True)
+    lanes = iota((ROWS, 128), 1)
+    xs[...] = jnp.zeros_like(xs)
+    xs[0:ROWS, :] = jnp.where(lanes == 0, top, jnp.where(lanes == 1, total, 0.0))
+    xt = xs[...].T
+    stats[0, :, 0:128] = xt[0:1, :]
+    stats[0, :, 128:256] = xt[1:2, :]
+
     pl.semaphore_wait(barrier, PEERS - 1 + CLS - 1)
 
     def peer_at(j):
@@ -126,9 +154,9 @@
         table_copy(j, 1).start()
         return carry
 
-    lax.fori_loop(1, PEERS, send_table, 0)
 
     y_up, y_down = {"img": z * 4 + lax.rem(y + 1, 4)}, {"img": z * 4 + lax.rem(y + 3, 4)}
+    y_far = {"img": z * 4 + lax.rem(y + 2, 4)}
     z_up, z_down = {"img": lax.rem(z + 1, 8) * 4 + y}, {"img": lax.rem(z + 7, 8) * 4 + y}
     sibling = {"cls": c + 1 - 2 * h}
     made = {}
@@ -148,98 +176,121 @@
             made[name].wait_recv()
 
     def at_a(zi, yi=0):
-        return A_BASE + 512 * h + 64 * zi + 16 * yi
+        return A_AT[zi][0] + A_AT[zi][1] * h + 16 * yi
 
     def at_b(yi, zi=0):
-        return B_BASE[yi] + 256 * h + 32 * zi
+        return B_AT[yi][zi][0] + B_AT[yi][zi][1] * h
 
     def share(name, at, n):
         go(name, at, at, n, sibling)
 
-    def round_0():
-        go("a_y2", at_a(0), at_a(0, 2), 16, y_up)
-        go("a_y1", at_a(0), at_a(0, 1), 16, y_down)
-        go("b_z2", at_b(0), at_b(0, 2), 32, z_up)
-        go("b_z1", at_b(0), at_b(0, 1), 32, z_down)
-
-    def round_1():
-        take("a_y1", "a_y2", "b_z1", "b_z2")
-        go("a_y3u", at_a(0, 2), at_a(0, 3), 16, y_up, slice(0, 512))
-        go("a_y3d", at_a(0, 1), at_a(0, 3), 16, y_down, slice(512, 1024))
-        go("b_z4", at_b(0, 2), at_b(0, 4), 32, z_up)
-        go("b_z3", at_b(0, 1), at_b(0, 3), 32, z_down)
-        go("b_y2q0", at_b(0), at_b(2), 96, y_up)
-        go("b_y1q0", at_b(0), at_b(1), 96, y_down)
-
-    def round_2():
-        take("a_y3u", "a_y3d", "b_z3", "b_z4")
-        go("a_z2", at_a(0), at_a(2), 64, z_up)
-        go("a_z1", at_a(0), at_a(1), 64, z_down)
-        go("b_z6", at_b(0, 4), at_b(0, 6), 32, z_up)
-        go("b_z5", at_b(0, 3), at_b(0, 5), 32, z_down)
-        share("a_s0", at_a(0, 1), 48)
-
-    def round_3():
-        take("b_z5", "b_z6")
-        go("b_z7u", at_b(0, 6), at_b(0, 7), 16, z_up)
-        go("b_z7d", at_b(0, 5) + 16, at_b(0, 7) + 16, 16, z_down)
-        take("a_z1", "a_z2")
-        go("a_z4", at_a(2), at_a(4), 64, z_up)
-        go("a_z3", at_a(1), at_a(3), 64, z_down)
-        share("a_s1", at_a(1), 128)
-
-    def round_4():
-        take("b_z7u", "b_z7d")
-        go("b_y2q1", at_b(0, 3), at_b(2, 3), 160, y_up)
-        go("b_y1q1", at_b(0, 3), at_b(1, 3), 160, y_down)
-        share("b_s0", at_b(0, 1), 224)
-        take("a_z3", "a_z4")
-        go("a_z6", at_a(4), at_a(6), 64, z_up)
-        go("a_z5", at_a(3), at_a(5), 64, z_down)
-        share("a_s3", at_a(3), 128)
-
-    def round_5():
-        take("b_y1q0", "b_y2q0")
-        go("b_y3q0u", at_b(2), at_b(3), 48, y_up)
-        go("b_y3q0d", at_b(1) + 48, at_b(3) + 48, 48, y_down)
-        take("a_z5", "a_z6")
-        go("a_z7u", at_a(6), at_a(7), 32, z_up)
-        go("a_z7d", at_a(5) + 32, at_a(7) + 32, 32, z_down)
-
-    def round_6():
-        take("a_z7u", "a_z7d")
-        share("a_s5", at_a(5), 192)
-
-    def round_7():
-        take("b_y1q1", "b_y2q1")
-        go("b_y3q1u", at_b(2, 3), at_b(3, 3), 80, y_up)
-        go("b_y3q1d", at_b(1, 3) + 80, at_b(3, 3) + 80, 80, y_down)
-        share("b_s1", at_b(1), 256)
-        share("b_s2", at_b(2), 256)
-
-    def round_8():
-        take("b_y3q0u", "b_y3q0d", "b_y3q1u", "b_y3q1d")
-        share("b_s3", at_b(3), 256)
-
-    round_0()
-
-    load_ct.wait()
-    column = c * N
-    top = jnp.full((ROWS, 1), -1e30, F32)
-    for off, width in TILES:
-        logits = dot_nt(e_ref[...], ct[off : off + width, :])
-        logits = jnp.where(column + off + iota((ROWS, width), 1) < LIVE, logits, -1e30)
-        buf1[0:ROWS, off : off + width] = logits
-        top = jnp.maximum(top, jnp.max(logits, axis=1, keepdims=True))
-    round_1()
-    total = jnp.zeros((ROWS, 1), F32)
-    for off, width in TILES:
-        total += jnp.sum(jnp.exp(buf1[0:ROWS, off : off + width] - top), axis=1, keepdims=True)
-    lanes = iota((ROWS, 128), 1)
-    xs[...] = jnp.zeros_like(xs)
-    xs[0:ROWS, :] = jnp.where(lanes == 0, top, jnp.where(lanes == 1, total, 0.0))
-    stats[0] = xs[...].T[:8, :]
-
+    LEFT, RIGHT = slice(0, 512), slice(512, 1024)
+
+    def a_hop(kind, at, n, old, new):
+        go(f"a{kind}{new + 1}", at_a(old + 1) + at, at_a(new + 1) + at, n, z_up)
+        go(f"a{kind}{new}", at_a(old) + at, at_a(new) + at, n, z_down)
+
+    def a_first(kind, at, n):
+        go(f"a{kind}2", at_a(0) + at, at_a(2) + at, n, z_up)
+        go(f"a{kind}1", at_a(0) + at, at_a(1) + at, n, z_down)
+
+    def a_next(kind, at, n, old):
+        take(f"a{kind}{old}", f"a{kind}{old + 1}")
+        a_hop(kind, at, n, old, old + 2)
+
+    def a_last(kind, at, n):
+        take(f"a{kind}5", f"a{kind}6")
+        go(f"a{kind}7u", at_a(6) + at, at_a(7) + at, n, z_up, LEFT)
+        go(f"a{kind}7d", at_a(5) + at, at_a(7) + at, n, z_down, RIGHT)
+
+    P_ROWS, Q_ROWS = (0, 16), (16, 48)
+
+    def b_next(old):
+        take(f"bz{old}", f"bz{old + 1}")
+        go(f"bz{old + 3}", at_b(0, old + 1), at_b(0, old + 3), 32, z_up)
+        go(f"bz{old + 2}", at_b(0, old), at_b(0, old + 2), 32, z_down)
+
+    def b_side(first, last):
+        n = 32 * (last - first)
+        go(f"by2{first}", at_b(0, first), at_b(2, first), n, y_up)
+        go(f"by1{first}", at_b(0, first), at_b(1, first), n, y_down)
+
+    def b_across(first, last):
+        n = 16 * (last - first)
+        take(f"by1{first}", f"by2{first}")
+        go(f"by3{first}u", at_b(2, first), at_b(3, first), n, y_up)
+        go(f"by3{first}d", at_b(1, first) + n, at_b(3, first) + n, n, y_down)
+
+    def events_0():
+        go("bz2", at_b(0), at_b(0, 2), 32, z_up)
+        go("bz1", at_b(0), at_b(0, 1), 32, z_down)
+        go("ay2", at_a(0), at_a(0, 2), 16, y_up)
+        go("ay1", at_a(0), at_a(0, 1), 16, y_down)
+        a_first("p", *P_ROWS)
+        go("ay3", at_a(0), at_a(0, 3), 16, y_far)
+
+    def events_1():
+        b_next(1)
+        b_side(0, 3)
+        a_next("p", *P_ROWS, 1)
+        take("ay1", "ay2", "ay3")
+        a_first("q", *Q_ROWS)
+        share("s0", at_b(0, 1), 64)
+        share("r0", at_a(0, 1), 48)
+
+    def events_2():
+        b_next(3)
+        b_side(3, 5)
+        a_next("p", *P_ROWS, 3)
+        share("s1", at_b(0, 3), 64)
+
+    def events_3():
+        take("bz5", "bz6")
+        go("bz7u", at_b(0, 6), at_b(0, 7), 16, z_up)
+        go("bz7d", at_b(0, 5) + 16, at_b(0, 7) + 16, 16, z_down)
+        b_side(5, 7)
+        share("s2", at_b(0, 5), 64)
+        a_next("q", *Q_ROWS, 1)
+        a_last("p", *P_ROWS)
+        b_across(0, 3)
+        share("r1", at_a(1), 128)
+        share("t10", at_b(1), 96)
+        share("t20", at_b(2), 96)
+
+    def events_4():
+        take("bz7u", "bz7d")
+        b_side(7, 8)
+        a_next("q", *Q_ROWS, 3)
+        b_across(3, 5)
+        share("s3", at_b(0, 7), 32)
+        share("r3", at_a(3), 128)
+        share("t13", at_b(1, 3), 64)
+        share("t23", at_b(2, 3), 64)
+
+    def events_5():
+        b_across(5, 7)
+        a_last("q", *Q_ROWS)
+        share("r5", at_a(5), 128)
+        share("t15", at_b(1, 5), 64)
+        share("t25", at_b(2, 5), 64)
+
+    def events_6():
+        b_across(7, 8)
+        take("ap7u", "ap7d", "aq7u", "aq7d")
+        share("r7", at_a(7), 64)
+        share("t17", at_b(1, 7), 32)
+        share("t27", at_b(2, 7), 32)
+
+    def events_7():
+        take("by33u", "by33d", "by35u", "by35d")
+        share("t33", at_b(3, 3), 128)
+
+    def events_8():
+        take("by30u", "by30d", "by37u", "by37d")
+        share("t30", at_b(3), 96)
+        share("t37", at_b(3, 7), 32)
+
+    lax.fori_loop(1, PEERS, send_table, 0)
     def stat_copy(j, n):
         src = stats.at[0] if n == 1 else stats.at[pl.ds(j, n)]
         dst = stats.at[j] if n == 1 else stats.at[pl.ds(j, n)]
@@ -252,7 +303,30 @@
         return carry
 
     lax.fori_loop(1, CLS, send_stat, 0)
-    round_2()
+    events_0()
+
+    stat_copy(1, CLS - 1).wait_recv()
+    top = stats[0, :, 0:128]
+    for j in range(1, CLS):
+        top = jnp.maximum(top, stats[j, :, 0:128])
+    total = jnp.zeros((1, 128), F32)
+    for j in range(CLS):
+        total += stats[j, :, 128:256] * jnp.exp(stats[j, :, 0:128] - top)
+    lses[0] = top + jnp.log(total)
+
+    def lse_copy(j, n):
+        src = lses.at[0] if n == 1 else lses.at[pl.ds(j, n)]
+        dst = lses.at[j] if n == 1 else lses.at[pl.ds(j, n)]
+        return pltpu.make_async_remote_copy(src, dst, lse_sem.at[0], lse_sem.at[1], device_id=peer_at(j), device_id_type=MESH)
+
+    def send_lse(j, carry):
+        lse_copy(j, 1).start()
+        return carry
+
+    lax.fori_loop(1, PEERS, send_lse, 0)
+
+    events_1()
+
 
     table_copy(1, PEERS - 1).wait_recv()
     mine = own[pl.ds(pl.multiple_of(HALF * h, 16), HALF), :]
@@ -292,27 +366,7 @@
     lists_a[...] = where >> 7
     lists_b[...] = where & 127
     lists_v[...] = jnp.where(itself, 1.0, values) * scale
-    round_3()
-
-    stat_copy(1, CLS - 1).wait_recv()
-    top = stats[0, 0:1, :]
-    for j in range(1, CLS):
-        top = jnp.maximum(top, stats[j, 0:1, :])
-    total = jnp.zeros((1, 128), F32)
-    for j in range(CLS):
-        total += stats[j, 1:2, :] * jnp.exp(stats[j, 0:1, :] - top)
-    lses[0] = top + jnp.log(total)
-
-    def lse_copy(j, n):
-        src = lses.at[0] if n == 1 else lses.at[pl.ds(j, n)]
-        dst = lses.at[j] if n == 1 else lses.at[pl.ds(j, n)]
-        return pltpu.make_async_remote_copy(src, dst, lse_sem.at[0], lse_sem.at[1], device_id=peer_at(j), device_id_type=MESH)
-
-    def send_lse(j, carry):
-        lse_copy(j, 1).start()
-        return carry
-
-    lax.fori_loop(1, PEERS, send_lse, 0)
+    events_2()
 
     def scatter(r, carry):
         a, b, v = lists_a[pl.ds(r, 1), :], lists_b[pl.ds(r, 1), :], lists_v[pl.ds(r, 1), :]
@@ -322,24 +376,23 @@
         dense[pl.ds(r, 24, stride=HALF), :] = out[:24] + out[32:56]
         return carry
 
-    lax.fori_loop(0, HALF, scatter, 0, unroll=8)
-    per = CHUNK // 128
+    lax.fori_loop(0, HALF // 2, scatter, 0, unroll=8)
+    events_3()
+    lax.fori_loop(HALF // 2, HALF, scatter, 0, unroll=8)
     mine_hi = pl.ds(pl.multiple_of(HALF * h, 16), HALF)
     mine_lo = pl.ds(pl.multiple_of(HALF * h + ROWS, 16), HALF)
-    for i in range(CHUNKS):
-        block = jnp.concatenate([dense[(per * i + j) * HALF : (per * i + j + 1) * HALF, :] for j in range(per)], axis=1)
-        hi, lo = split(block)
-        m_ref[i, mine_hi, :] = hi
-        m_ref[i, mine_lo, :] = lo
+    for i in range(ALL // 128):
+        hi, lo = split(dense[i * HALF : (i + 1) * HALF, :])
+        m_ref[mine_hi, i * 128 : (i + 1) * 128] = hi
+        m_ref[mine_lo, i * 128 : (i + 1) * 128] = lo
     m_copies = [
         pltpu.make_async_remote_copy(
-            m_ref.at[:, part, :], m_ref.at[:, part, :], m_sem.at[i, 0], m_sem.at[i, 1], device_id=sibling, device_id_type=MESH
+            m_ref.at[part], m_ref.at[part], m_sem.at[i, 0], m_sem.at[i, 1], device_id=sibling, device_id_type=MESH
         )
         for i, part in enumerate((mine_hi, mine_lo))
     ]
     for copy in m_copies:
         copy.start()
-    round_4()
 
     lse_copy(1, PEERS - 1).wait_recv()
     xs[...] = jnp.zeros_like(xs)
@@ -351,39 +404,54 @@
             yi = dy if dy < 2 else 5 - dy
             for half in range(2):
                 col = jnp.broadcast_to(ys[HALF * half : HALF * half + HALF, dz * 4 + dy : dz * 4 + dy + 1], (HALF, 128))
-                a = A_BASE + 512 * half + 64 * zi + 16 * yi
-                b = B_BASE[yi] + 256 * half + 32 * zi
+                a = A_AT[zi][0] + A_AT[zi][1] * half + 16 * yi
+                b = B_AT[yi][zi][0] + B_AT[yi][zi][1] * half
                 lse_ref[a : a + 16, :] = col[:16]
                 lse_ref[b : b + 32, :] = col[16:]
     acc[...] = jnp.zeros_like(acc)
-    round_5()
-    take("b_s0")
-
     def logits_tile(chunk, off, width):
-        bufs[chunk % 2][:, off : off + width] = dot_nt(every[chunk * CHUNK : (chunk + 1) * CHUNK, :], ct[off : off + width, :])
+        first, last = CHUNK_AT[chunk], CHUNK_AT[chunk + 1]
+        bufs[chunk % 2][: last - first, off : off + width] = dot_nt(every[first:last, :], ct[off : off + width, :])
 
     def label_tile(chunk, off, width):
-        lse = lse_ref[chunk * CHUNK : (chunk + 1) * CHUNK, :]
+        first, last = CHUNK_AT[chunk], CHUNK_AT[chunk + 1]
+        lse = lse_ref[first:last, :]
         lse = jnp.concatenate([lse] * (-(-width // 128)), axis=1)[:, :width]
-        hi, lo = split(jnp.exp(bufs[chunk % 2][:, off : off + width] - lse))
-        m = m_ref[chunk]
+        hi, lo = split(jnp.exp(bufs[chunk % 2][: last - first, off : off + width] - lse))
+        m = m_ref[:, first:last]
         a = dot(m, hi)
         acc[:, off : off + width] += a[:ROWS] + a[ROWS:] + dot(m[:ROWS], lo)
 
-    for off, width in TILES:
-        logits_tile(0, off, width)
-    for copy in m_copies:
-        copy.wait_recv()
-    round_6()
-    take("a_s0", "a_s1", "a_s3", "a_s5")
-    before = {0: [], 1: [round_7], 2: [round_8, lambda: take("b_s1")], 3: [lambda: take("b_s2")], 4: [lambda: take("b_s3")]}
-    for chunk in range(CHUNKS):
-        for event in before.get(chunk, []):
-            event()
-        for off, width in TILES:
+    def wait_matrix():
+        for copy in m_copies:
+            copy.wait_recv()
+
+    arrivals = [
+        ("r0", "s0", "s1", "s2"),
+        ("r1", "t10", "t20"),
+        ("s3", "r3", "t13", "t23"),
+        ("r5", "t15", "t25"),
+        ("r7", "t17", "t27", "t33"),
+        ("t30", "t37"),
+    ]
+    events = {
+        (-1, 5): events_4,
+        (0, 0): wait_matrix,
+        (0, 5): events_5,
+        (1, 4): events_6,
+        (2, 0): events_7,
+        (2, 8): events_8,
+    }
+    for chunk in range(-1, CHUNKS):
+        if chunk + 1 < CHUNKS:
+            take(*arrivals[chunk + 1])
+        for i, (off, width) in enumerate(TILES):
+            if (chunk, i) in events:
+                events[chunk, i]()
             if chunk + 1 < CHUNKS:
                 logits_tile(chunk + 1, off, width)
-            label_tile(chunk, off, width)
+            if chunk >= 0:
+                label_tile(chunk, off, width)
     for off, width in TILES:
         here = column + off + iota((ROWS, width), 1)
         o_ref[:, off : off + width] = jnp.where(here < LIVE, acc[:, off : off + width], 0.0)
@@ -412,7 +480,7 @@
             pltpu.VMEM((CHUNK, N), F32),
             pltpu.VMEM((ROWS, N), F32),
             pltpu.VMEM((ALL, 128), F32),
-            pltpu.VMEM((CHUNKS, 2 * ROWS, CHUNK), BF16),
+            pltpu.VMEM((2 * ROWS, ALL), BF16),
             pltpu.VMEM((24 * HALF, 128), F32),
             pltpu.VMEM((PACK, 128), BF16),
             pltpu.VMEM((PEERS * PACK, 128), BF16),
@@ -423,7 +491,7 @@
             pltpu.VMEM((HALF, 128), jnp.int32),
             pltpu.VMEM((HALF, 128), F32),
             pltpu.VMEM((K * HALF, 128), F32),
-            pltpu.VMEM((CLS, 8, 128), F32),
+            pltpu.VMEM((CLS, 1, 256), F32),
             pltpu.VMEM((PEERS, 1, 128), F32),
             dma,
             dma((MESSAGES,)),

time: 75.1 us -> 65.4 us (0.87)
  Pallas kernels: 72.6 us -> 62.7 us
    pallas_call x1, Pallas kernels: 72.6 us -> 62.7 us  [shards(): pl.pallas_call(kernel, out_shape=jax.ShapeDtypeStruct((ROWS, N), F32), in...]
where the time goes in v3:
time: 65.4 us; the launch traced here: 65 us
  Pallas kernels  62.7 us (96%)
  local copies, waits for them, and re-layouts  2.29 us (4%)
    pallas_call x1, Pallas kernels, shards(): pl.pallas_call(kernel, out_shape=jax.ShapeDtypeStruct((ROWS, N), F32), in...  62.7 us
    unnamed x1, local copies, waits for them, and re-layouts  2.29 us

profile of v3, /device:TPU:1, one launch (start us, length us, event | category | flops | bytes accessed | tf_op | source)
XLA Modules:
  0.0 65.0 jit_solution(5208463978777050001)
XLA Ops:
  0.0 62.7 %shard_map.55 = f32[96,2736]{1,0:T(8,128)} custom-call(bf16[96,1024]{1,0:T(8,128)(2,1)} %e_ref.1, bf16[2736,1024]{1,0:T(8,128)(2,1)} %bitcast.6, s32[10,96]{1,0:T(8,128)} %bitcast.7, f32[10,96]{1,0:T(8,128)} %bitcast.8, s32[16,32]{1,0:T(8,128)} %bitcast.9), custom_call_target="tpu_custom_call" | custom-call | tf_op jit(solution)/shard_map/pallas_call | solution.py:471
  62.7 2.3 %copy.7 = f32[96,2736]{1,0:T(8,128)} copy(f32[96,2736]{1,0:T(8,128)} %shard_map.55) | data formatting | bytes 2101248

commit v4 on v3

--- a/solution.py
+++ b/solution.py
@@ -20,14 +20,14 @@
 BF16 = jnp.bfloat16
 MESH = pl.DeviceIdType.MESH
 TILES = [(off, min(TN, N - off)) for off in range(0, N, TN)]
-A_AT = [(0, 1152)] + [(s + 64 * i, 128) for s in (512, 1280, 1792) for i in range(2)] + [(2304, 64)]
+A_AT = [(0, 64)] + [(s + 64 * i, 128) for s in (384, 1280, 1664) for i in range(2)] + [(2304, 64)]
 B_AT = [
-    [(64 + 32 * i, 224) for i in range(7)] + [(1216, 32)],
-    [(768 + 32 * i, 96) for i in range(3)] + [(s + 32 * i, 64) for s in (1536, 2048) for i in range(2)] + [(2432, 32)],
-    [(960 + 32 * i, 96) for i in range(3)] + [(s + 32 * i, 64) for s in (1664, 2176) for i in range(2)] + [(2496, 32)],
-    [(2816 + 32 * i, 96) for i in range(3)] + [(2560 + 32 * i, 128) for i in range(4)] + [(3008, 32)],
+    [(128 + 32 * i, 128) for i in range(4)] + [(1024 + 32 * i, 128) for i in range(4)],
+    [(640 + 32 * i, 96) for i in range(3)] + [(1536, 32)] + [(1920 + 32 * i, 96) for i in range(3)] + [(2432, 32)],
+    [(832 + 32 * i, 96) for i in range(3)] + [(1600, 32)] + [(2112 + 32 * i, 96) for i in range(3)] + [(2496, 32)],
+    [(2560 + 32 * i, 96) for i in range(3)] + [(2752, 32)] + [(2816 + 32 * i, 96) for i in range(3)] + [(3008, 32)],
 ]
-CHUNK_AT = (0, 512, 1152, 1792, 2304, 2816, 3072)
+CHUNK_AT = (0, 384, 1024, 1664, 2304, 2816, 3072)
 CHUNKS = 6
 CHUNK = 640
 MESSAGES = 72
@@ -70,7 +70,7 @@
 
 def kernel(
     e_ref, ct_hbm, near_ref, w_ref, ask_ref, o_ref,
-    every, ct, buf0, buf1, acc, lse_ref, m_ref, dense, table, all_tables, own, xs, ys, lists_a, lists_b, lists_v, got, stats, lses,
+    every, ct, buf0, buf1, lse_ref, m_ref, dense, table, all_tables, own, xs, ys, lists_a, lists_b, lists_v, hots, got, stats, lses,
     ct_sem, ssem, rsem, table_sem, stat_sem, lse_sem, m_sem,
 ):
     me, c = lax.axis_index("img"), lax.axis_index("cls")
@@ -119,7 +119,7 @@
             at = q * 4 * K + i * K
             xs[at : at + K, 0:PACK] = piece[:, q * PACK : (q + 1) * PACK]
     table[...] = xs[...].T[:PACK, :].astype(BF16)
-    all_tables[0:PACK, :] = table[...]
+    all_tables[0] = table[...]
     own[...] = ys[...].T
 
     load_ct.wait()
@@ -140,15 +140,31 @@
     stats[0, :, 0:128] = xt[0:1, :]
     stats[0, :, 128:256] = xt[1:2, :]
 
+
+    mine = own[pl.ds(pl.multiple_of(HALF * h, 16), HALF), :]
+    lanes = iota((HALF, 128), 1)
+    peer = mine.astype(jnp.int32)
+    row = pltpu.roll(mine, 128 - 16, 1).astype(jnp.int32)
+    weight = pltpu.roll(mine, 128 - 32, 1)
+    scale = 1.0 / (1.0 + jnp.sum(jnp.where(lanes < K, weight, 0.0), axis=1, keepdims=True))
+    dz, dy = relative(z, y, peer)
+    packed = (dz * 4 + dy) * PACK + (row & (PACK - 1))
+    group = row >> 5
+    for k in range(K):
+        at = iota((HALF, PEERS * PACK), 1)
+        hots[k * HALF : (k + 1) * HALF, :] = jnp.where(at == packed[:, k : k + 1], 1.0, 0.0).astype(BF16)
+
     pl.semaphore_wait(barrier, PEERS - 1 + CLS - 1)
 
     def peer_at(j):
         return {"img": lax.rem(z + 8 - j // 4, 8) * 4 + lax.rem(y + 4 - lax.rem(j, 4), 4)}
 
+    table_half = pl.ds(pl.multiple_of(h * (PACK // 2), 16), PACK // 2)
+
     def table_copy(j, n):
-        rows = pl.ds(pl.multiple_of(j * PACK, PACK), n * PACK)
-        src = table if n == 1 else all_tables.at[rows]
-        return pltpu.make_async_remote_copy(src, all_tables.at[rows], table_sem.at[0], table_sem.at[1], device_id=peer_at(j), device_id_type=MESH)
+        src = table.at[table_half] if n == 1 else all_tables.at[pl.ds(j, n), table_half]
+        dst = all_tables.at[j, table_half] if n == 1 else all_tables.at[pl.ds(j, n), table_half]
+        return pltpu.make_async_remote_copy(src, dst, table_sem.at[0], table_sem.at[1], device_id=peer_at(j), device_id_type=MESH)
 
     def send_table(j, carry):
         table_copy(j, 1).start()
@@ -240,39 +256,39 @@
 
     def events_2():
         b_next(3)
-        b_side(3, 5)
+        b_side(3, 4)
+        share("s1", at_b(0, 3), 32)
         a_next("p", *P_ROWS, 3)
-        share("s1", at_b(0, 3), 64)
 
     def events_3():
         take("bz5", "bz6")
         go("bz7u", at_b(0, 6), at_b(0, 7), 16, z_up)
         go("bz7d", at_b(0, 5) + 16, at_b(0, 7) + 16, 16, z_down)
-        b_side(5, 7)
-        share("s2", at_b(0, 5), 64)
+        b_side(4, 7)
         a_next("q", *Q_ROWS, 1)
         a_last("p", *P_ROWS)
         b_across(0, 3)
         share("r1", at_a(1), 128)
         share("t10", at_b(1), 96)
         share("t20", at_b(2), 96)
+        share("s2", at_b(0, 4), 96)
 
     def events_4():
         take("bz7u", "bz7d")
         b_side(7, 8)
         a_next("q", *Q_ROWS, 3)
-        b_across(3, 5)
+        b_across(3, 4)
+        share("r3", at_a(3), 128)
+        share("t13", at_b(1, 3), 32)
+        share("t23", at_b(2, 3), 32)
         share("s3", at_b(0, 7), 32)
-        share("r3", at_a(3), 128)
-        share("t13", at_b(1, 3), 64)
-        share("t23", at_b(2, 3), 64)
 
     def events_5():
-        b_across(5, 7)
+        b_across(4, 7)
         a_last("q", *Q_ROWS)
         share("r5", at_a(5), 128)
-        share("t15", at_b(1, 5), 64)
-        share("t25", at_b(2, 5), 64)
+        share("t14", at_b(1, 4), 96)
+        share("t24", at_b(2, 4), 96)
 
     def events_6():
         b_across(7, 8)
@@ -282,12 +298,13 @@
         share("t27", at_b(2, 7), 32)
 
     def events_7():
-        take("by33u", "by33d", "by35u", "by35d")
-        share("t33", at_b(3, 3), 128)
+        take("by30u", "by30d", "by33u", "by33d")
+        share("t30", at_b(3), 96)
+        share("t33", at_b(3, 3), 32)
 
     def events_8():
-        take("by30u", "by30d", "by37u", "by37d")
-        share("t30", at_b(3), 96)
+        take("by34u", "by34d", "by37u", "by37d")
+        share("t34", at_b(3, 4), 96)
         share("t37", at_b(3, 7), 32)
 
     lax.fori_loop(1, PEERS, send_table, 0)
@@ -325,24 +342,14 @@
 
     lax.fori_loop(1, PEERS, send_lse, 0)
 
+
+    table_copy(1, PEERS - 1).wait_recv()
+    others = all_tables.at[pl.ds(1, PEERS - 1), table_half]
+    table_share = pltpu.make_async_remote_copy(others, others, table_sem.at[2], table_sem.at[3], device_id=sibling, device_id_type=MESH)
+    table_share.start()
     events_1()
-
-
-    table_copy(1, PEERS - 1).wait_recv()
-    mine = own[pl.ds(pl.multiple_of(HALF * h, 16), HALF), :]
-    lanes = iota((HALF, 128), 1)
-    peer = mine.astype(jnp.int32)
-    row = pltpu.roll(mine, 128 - 16, 1).astype(jnp.int32)
-    weight = pltpu.roll(mine, 128 - 32, 1)
-    scale = 1.0 / (1.0 + jnp.sum(jnp.where(lanes < K, weight, 0.0), axis=1, keepdims=True))
-    dz, dy = relative(z, y, peer)
-    packed = (dz * 4 + dy) * PACK + (row & (PACK - 1))
-    group = row >> 5
-    for step in range(4):
-        at = iota((HALF, 256), 1) + step * 256
-        hot = [jnp.where(at == packed[:, k : k + 1], 1.0, 0.0).astype(BF16) for k in range(K)]
-        part = dot(jnp.concatenate(hot, axis=0), all_tables[step * 256 : step * 256 + 256, :])
-        got[...] = part if step == 0 else got[...] + part
+    table_share.wait_recv()
+    got[...] = dot(hots[...], jnp.concatenate([all_tables[j] for j in range(PEERS)], axis=0))
     peers = jnp.zeros((HALF, 128), F32)
     rows = jnp.zeros((HALF, 128), F32)
     values = jnp.zeros((HALF, 128), F32)
@@ -376,9 +383,7 @@
         dense[pl.ds(r, 24, stride=HALF), :] = out[:24] + out[32:56]
         return carry
 
-    lax.fori_loop(0, HALF // 2, scatter, 0, unroll=8)
-    events_3()
-    lax.fori_loop(HALF // 2, HALF, scatter, 0, unroll=8)
+    lax.fori_loop(0, HALF, scatter, 0, unroll=24)
     mine_hi = pl.ds(pl.multiple_of(HALF * h, 16), HALF)
     mine_lo = pl.ds(pl.multiple_of(HALF * h + ROWS, 16), HALF)
     for i in range(ALL // 128):
@@ -398,17 +403,19 @@
     xs[...] = jnp.zeros_like(xs)
     xs[0:PEERS, :] = lses[:, 0, :]
     ys[...] = xs[...].T
-    for dz in range(8):
-        for dy in range(4):
-            zi = 0 if dz == 0 else 2 * dz - 1 if dz <= 4 else 16 - 2 * dz
-            yi = dy if dy < 2 else 5 - dy
-            for half in range(2):
-                col = jnp.broadcast_to(ys[HALF * half : HALF * half + HALF, dz * 4 + dy : dz * 4 + dy + 1], (HALF, 128))
-                a = A_AT[zi][0] + A_AT[zi][1] * half + 16 * yi
-                b = B_AT[yi][zi][0] + B_AT[yi][zi][1] * half
-                lse_ref[a : a + 16, :] = col[:16]
-                lse_ref[b : b + 32, :] = col[16:]
-    acc[...] = jnp.zeros_like(acc)
+
+    def expand(j):
+        dz, dy = j // 4, j % 4
+        zi = 0 if dz == 0 else 2 * dz - 1 if dz <= 4 else 16 - 2 * dz
+        yi = dy if dy < 2 else 5 - dy
+        for half in range(2):
+            col = jnp.broadcast_to(ys[HALF * half : HALF * half + HALF, j : j + 1], (HALF, 128))
+            a = A_AT[zi][0] + A_AT[zi][1] * half + 16 * yi
+            b = B_AT[yi][zi][0] + B_AT[yi][zi][1] * half
+            lse_ref[a : a + 16, :] = col[:16]
+            lse_ref[b : b + 32, :] = col[16:]
+
+    o_ref[...] = jnp.zeros_like(o_ref)
     def logits_tile(chunk, off, width):
         first, last = CHUNK_AT[chunk], CHUNK_AT[chunk + 1]
         bufs[chunk % 2][: last - first, off : off + width] = dot_nt(every[first:last, :], ct[off : off + width, :])
@@ -420,27 +427,28 @@
         hi, lo = split(jnp.exp(bufs[chunk % 2][: last - first, off : off + width] - lse))
         m = m_ref[:, first:last]
         a = dot(m, hi)
-        acc[:, off : off + width] += a[:ROWS] + a[ROWS:] + dot(m[:ROWS], lo)
+        o_ref[:, off : off + width] += a[:ROWS] + a[ROWS:] + dot(m[:ROWS], lo)
 
     def wait_matrix():
         for copy in m_copies:
             copy.wait_recv()
 
     arrivals = [
-        ("r0", "s0", "s1", "s2"),
+        ("r0", "s0", "s1"),
         ("r1", "t10", "t20"),
-        ("s3", "r3", "t13", "t23"),
-        ("r5", "t15", "t25"),
-        ("r7", "t17", "t27", "t33"),
-        ("t30", "t37"),
+        ("s2", "s3", "r3", "t13", "t23"),
+        ("r5", "t14", "t24"),
+        ("r7", "t17", "t27", "t30", "t33"),
+        ("t34", "t37"),
     ]
     events = {
-        (-1, 5): events_4,
+        (-1, 6): events_3,
         (0, 0): wait_matrix,
-        (0, 5): events_5,
-        (1, 4): events_6,
-        (2, 0): events_7,
-        (2, 8): events_8,
+        (0, 6): events_4,
+        (1, 5): events_5,
+        (2, 2): events_6,
+        (2, 6): events_7,
+        (3, 2): events_8,
     }
     for chunk in range(-1, CHUNKS):
         if chunk + 1 < CHUNKS:
@@ -452,15 +460,15 @@
                 logits_tile(chunk + 1, off, width)
             if chunk >= 0:
                 label_tile(chunk, off, width)
-    for off, width in TILES:
-        here = column + off + iota((ROWS, width), 1)
-        o_ref[:, off : off + width] = jnp.where(here < LIVE, acc[:, off : off + width], 0.0)
-
+            else:
+                for j in range(3 * i, min(3 * i + 3, PEERS)):
+                    expand(j)
     for copy in made.values():
         copy.wait_send()
     for copy in m_copies:
         copy.wait_send()
     table_copy(1, PEERS - 1).wait_send()
+    table_share.wait_send()
     stat_copy(1, CLS - 1).wait_send()
     lse_copy(1, PEERS - 1).wait_send()
 
@@ -468,7 +476,8 @@
 def shards(embeddings, class_text_embedding, neighbours, weights, requests):
     vmem = pl.BlockSpec(memory_space=pltpu.VMEM)
     dma = pltpu.SemaphoreType.DMA
-    return pl.pallas_call(
+    live = lax.axis_index("cls") * N + jnp.arange(N) < LIVE
+    labels = pl.pallas_call(
         kernel,
         out_shape=jax.ShapeDtypeStruct((ROWS, N), F32),
         in_specs=[vmem, pl.BlockSpec(memory_space=pl.ANY), vmem, vmem, vmem],
@@ -478,31 +487,32 @@
             pltpu.VMEM((N, D), BF16),
             pltpu.VMEM((CHUNK, N), F32),
             pltpu.VMEM((CHUNK, N), F32),
-            pltpu.VMEM((ROWS, N), F32),
             pltpu.VMEM((ALL, 128), F32),
             pltpu.VMEM((2 * ROWS, ALL), BF16),
             pltpu.VMEM((24 * HALF, 128), F32),
             pltpu.VMEM((PACK, 128), BF16),
-            pltpu.VMEM((PEERS * PACK, 128), BF16),
+            pltpu.VMEM((PEERS, PACK, 128), BF16),
             pltpu.VMEM((128, 128), F32),
             pltpu.VMEM((128, 128), F32),
             pltpu.VMEM((128, 128), F32),
             pltpu.VMEM((HALF, 128), jnp.int32),
             pltpu.VMEM((HALF, 128), jnp.int32),
             pltpu.VMEM((HALF, 128), F32),
+            pltpu.VMEM((K * HALF, PEERS * PACK), BF16),
             pltpu.VMEM((K * HALF, 128), F32),
             pltpu.VMEM((CLS, 1, 256), F32),
             pltpu.VMEM((PEERS, 1, 128), F32),
             dma,
             dma((MESSAGES,)),
             dma((MESSAGES,)),
-            dma((2,)),
+            dma((4,)),
             dma((2,)),
             dma((2,)),
             dma((2, 2)),
         ],
         compiler_params=pltpu.CompilerParams(vmem_limit_bytes=56 << 20, collective_id=0, has_side_effects=True),
     )(embeddings, class_text_embedding.T, neighbours.T, weights.T, requests[0].T)
+    return jnp.where(live[None, :], labels, 0.0)
 
 
 def solution(mesh):

time: 65.4 us -> 61.4 us (0.939)
  Pallas kernels: 62.7 us -> 58.9 us
  other arithmetic: 0 us -> 2.3 us
  local copies, waits for them, and re-layouts: 2.29 us -> 0 us
    pallas_call x1, Pallas kernels: 62.7 us -> 58.9 us  [shards(): pl.pallas_call(kernel, out_shape=jax.ShapeDtypeStruct((ROWS, N), F32), in...]
    select_n x0 -> x1, other arithmetic: none -> 2.3 us  [shards(): return jnp.where(live[None, :], labels, 0.0)]
    unnamed x1 -> x0, local copies, waits for them, and re-layouts: 2.29 us -> none
where the time goes in v4:
time: 61.4 us; the launch traced here: 61.2 us
  Pallas kernels  58.9 us (96%)
  other arithmetic  2.3 us (4%)
    pallas_call x1, Pallas kernels, shards(): pl.pallas_call(kernel, out_shape=jax.ShapeDtypeStruct((ROWS, N), F32), in...  58.9 us
    select_n x1, other arithmetic, shards(): return jnp.where(live[None, :], labels, 0.0)  2.3 us

profile of v4, /device:TPU:1, one launch (start us, length us, event | category | flops | bytes accessed | tf_op | source)
XLA Modules:
  0.0 61.2 jit_solution(17222212804915995153)
XLA Ops:
  0.0 58.9 %shard_map.55 = f32[96,2736]{1,0:T(8,128)} custom-call(bf16[96,1024]{1,0:T(8,128)(2,1)} %e_ref.1, bf16[2736,1024]{1,0:T(8,128)(2,1)} %bitcast.6, s32[10,96]{1,0:T(8,128)} %bitcast.7, f32[10,96]{1,0:T(8,128)} %bitcast.8, s32[16,32]{1,0:T(8,128)} %bitcast.9), custom_call_target="tpu_custom_call" | custom-call | tf_op jit(solution)/shard_map/pallas_call | solution.py:480
  58.9 2.3 %broadcast_select_fusion = f32[96,2736]{1,0:T(8,128)} fusion(f32[96,2736]{1,0:T(8,128)} %shard_map.55, pred[2736]{0:T(1024)(128)(4,1)S(1)} %add_compare_fusion), kind=kLoop, calls=%fused_computation | loop fusion | flops 262656 | bytes 2103984 | tf_op jit(solution)/shard_map/jit(_where)/select_n | solution.py:515
  (1 shorter events, 0.0 us)
